TPU v7x, 32 devices: a whole 2x2x4 slice. The times are simulated.
32 devices in a mesh: fsdp: 8 (over y, x, core), rep: 4 (over z).
Axes of the slice: x: 2, y: 2, z: 4, core: 2. Of those that a mesh axis runs over, the one named last changes fastest.
Arguments:
- inputs: bfloat16 [4, 1024, 4096], P('rep', 'fsdp'), may hold values from -6 to 6
- out_grad: bfloat16 [4, 1024, 512], P('rep', 'fsdp'), may hold values from -6 to 6
- weight: bfloat16 [4096, 512], P('fsdp'), may hold values from -6 to 6
- momentum: float32 [4, 512, 4096], P('rep', 'fsdp'), may hold values from -6 to 6
- band_index: int32 [128], replicated, may hold values from 0 to 511, as said below
Outputs:
- leftover: float32 [4, 512, 4096], P('rep', 'fsdp')
- new_weight: bfloat16 [4096, 512], P('fsdp')
- values: bfloat16 [4, 1024, 512], P('rep', 'fsdp')
Inputs may be any that keep to these rules, and one draw needn't show every extreme that they name: `band_index`: distinct entries below 512; 0 and 511 are always among them.
All inputs are finite; a program needn't handle non-finite values.
Results may differ from a plain program's by a relative error of at most 0.0049.
Values may be sent and summed in bfloat16 or wider, within the bound.
A program may use at most 64 MiB of HBM per device.

v0:
```python
import functools
import math

import jax
import jax.numpy as jnp
from jax import lax
from jax.experimental import pallas as pl
from jax.experimental.pallas import tpu as pltpu
from jax.sharding import PartitionSpec as P

MOMENTUM_DECAY = 0.9
LEARNING_RATE = 4.0


def dct_rows(band_index, length):
    positions = lax.iota(jnp.int32, length)
    phase_int = (2 * positions[None, :] + 1) * band_index[:, None] % (4 * length)
    angles = phase_int.astype(jnp.float32) * (math.pi / (2 * length))
    row_scale = jnp.where(band_index == 0, math.sqrt(1.0 / length), math.sqrt(2.0 / length)).astype(
        jnp.float32
    )
    return row_scale[:, None] * jnp.cos(angles)


def rebuild_rows(old_rows, update_rows):
    return (old_rows.astype(jnp.float32) - LEARNING_RATE * update_rows).astype(jnp.bfloat16)


def shards(inputs, out_grad, weight, momentum, band_index):
    tok_inputs = inputs[0]
    upstream = out_grad[0]
    own_rows = weight.shape[0]
    width_out = weight.shape[1]
    group_len = momentum.shape[2]
    scaling = 1.0 / math.sqrt(tok_inputs.shape[1])
    highest = lax.Precision.HIGHEST
    own_columns = lax.all_to_all(tok_inputs, "fsdp", split_axis=1, concat_axis=0, tiled=True)
    gradient = (
        lax.dot_general(
            own_columns,
            lax.all_gather(upstream, "fsdp", axis=0, tiled=True),
            (((0,), (0,)), ((), ())),
            preferred_element_type=jnp.float32,
        )
        * scaling
    )
    moment = MOMENTUM_DECAY * momentum[0] + gradient.reshape(-1, group_len)
    dct_basis = dct_rows(band_index, group_len)
    coeffs = jnp.dot(moment, dct_basis.T, precision=highest)
    leftover = (moment - jnp.dot(coeffs, dct_basis, precision=highest))[None]
    shared = lax.psum(coeffs, "rep") / lax.axis_size("rep")
    own_update = jnp.dot(shared, dct_basis, precision=highest).reshape(own_rows, width_out)
    new_weight = rebuild_rows(weight, own_update)
    running = jnp.dot(
        tok_inputs,
        lax.all_gather(new_weight, "fsdp", axis=0, tiled=True),
        preferred_element_type=jnp.float32,
    )
    values = (running * scaling).astype(jnp.bfloat16)[None]
    return (leftover, new_weight, values)


LANES = 128
F32, BF16 = jnp.float32, jnp.bfloat16


def split_hi_lo(x):
    hi = x.astype(BF16)
    return hi, (x - hi.astype(F32)).astype(BF16)


def dot(a, b, dims=((1,), (0,))):
    return lax.dot_general(a, b, (dims, ((), ())), preferred_element_type=F32)


def dot3(a_hi, a_lo, b_hi, b_lo, dims=((1,), (0,))):
    return dot(a_hi, b_hi, dims) + dot(a_hi, b_lo, dims) + dot(a_lo, b_hi, dims)


def fill_basis(band_ref, bh, bl, bt):
    slabs, bands, width = bh.shape
    length = slabs * width
    period = 4 * length
    freq = jnp.broadcast_to(band_ref[...].astype(F32), (LANES, bands)).T.astype(jnp.int32)
    lane = lax.broadcasted_iota(jnp.int32, (bands, LANES), 1)
    row_scale = jnp.where(freq == 0, math.sqrt(1.0 / length), math.sqrt(2.0 / length)).astype(F32)

    def angle(steps):
        centred = ((steps * freq + period // 2) & (period - 1)) - period // 2
        return centred.astype(F32) * (math.pi / (2 * length))

    fine, coarse = angle(2 * lane + 1), angle(2 * LANES * lane)
    cos_fine, sin_fine = row_scale * jnp.cos(fine), row_scale * jnp.sin(fine)
    cos_coarse, sin_coarse = jnp.cos(coarse), jnp.sin(coarse)
    for at in range(length // LANES):
        tile = cos_coarse[:, at : at + 1] * cos_fine - sin_coarse[:, at : at + 1] * sin_fine
        hi, lo = split_hi_lo(tile)
        a, col = divmod(at * LANES, width)
        bh[a, :, col : col + LANES] = hi
        bl[a, :, col : col + LANES] = lo
        hi, lo = split_hi_lo(tile.T)
        bt[at * LANES : (at + 1) * LANES, :bands] = hi
        bt[at * LANES : (at + 1) * LANES, bands:] = lo


def kernel(
    n, reps, band_ref, x_hbm, og_hbm, w_hbm, mom_hbm, left, nw, val,
    x, oc, og, w, mom, bh, bl, bt, perm, xa, grad, upd, odd, even, pin, pout, vin, cz, sg,
    load_sem, oc_send, oc_recv, og_send, og_recv, r_send, r_recv, p_send, p_recv, v_send, v_recv,
    c_send, c_recv, s_send, s_recv,
):
    me, rep = lax.axis_index("fsdp"), lax.axis_index("rep")
    tokens, depth = x.shape
    own_rows, width = w.shape
    slabs, bands, _ = bh.shape
    groups = mom.shape[0]
    scaling = 1.0 / math.sqrt(depth)
    bits = n.bit_length() - 1

    def peer(k):
        return sum((((me // 2**b) % 2 + (k >> b) % 2) % 2) * 2**b for b in range(bits))

    def across(d):
        return lax.rem(rep + d, reps)

    def columns(which):
        return pl.ds(pl.multiple_of(which * own_rows, LANES), own_rows)

    def to_peer(k, src, dst, send, recv):
        return pltpu.make_async_remote_copy(
            src_ref=src, dst_ref=dst, send_sem=send, recv_sem=recv,
            device_id={"fsdp": peer(k)}, device_id_type=pl.DeviceIdType.MESH,
        )

    def to_rep(d, src, dst, send, recv):
        return pltpu.make_async_remote_copy(
            src_ref=src, dst_ref=dst, send_sem=send, recv_sem=recv,
            device_id={"rep": across(d)}, device_id_type=pl.DeviceIdType.MESH,
        )

    loads = [
        pltpu.make_async_copy(x_hbm.at[0], x, load_sem.at[0]),
        pltpu.make_async_copy(og_hbm.at[0], og.at[0], load_sem.at[1]),
        pltpu.make_async_copy(w_hbm, w, load_sem.at[2]),
        pltpu.make_async_copy(mom_hbm.at[0], mom, load_sem.at[3]),
        pltpu.make_async_copy(x_hbm.at[0, :, columns(me)], oc.at[0], load_sem.at[4]),
    ]
    for load in loads:
        load.start()

    barrier = pltpu.get_barrier_semaphore()
    for d in range(1, reps):
        pl.semaphore_signal(
            barrier, inc=1, device_id={"rep": across(d)}, device_id_type=pl.DeviceIdType.MESH
        )
    for k in range(n - 1, 0, -1):
        pl.semaphore_signal(
            barrier, inc=1, device_id={"fsdp": peer(k)}, device_id_type=pl.DeviceIdType.MESH
        )
    pl.semaphore_wait(barrier, n - 1 + reps - 1)

    def crossings(k):
        return bin(k >> 1).count("1")

    relayed = [k for k in range(2, n, 2) if crossings(k) == 2]
    direct = [k for k in range(2, n, 2) if k not in relayed]
    order = sorted(range(2, n), key=lambda k: (-crossings(k), 1 - k % 2, k))
    og_copies = {
        k: to_peer(k, og_hbm.at[0], og.at[k], og_send.at[k], og_recv.at[k]) for k in direct + [1]
    }
    oc_copies = {
        k: to_peer(k, x_hbm.at[0, :, columns(peer(k))], oc.at[k], oc_send.at[k], oc_recv.at[k])
        for k in range(1, n)
    }
    forward = {
        k: to_peer(1, og.at[k], og.at[k + 1], og_send.at[k + 1], og_recv.at[k + 1])
        for k in range(2, n, 2)
    }
    relays = {}
    for k in relayed:
        low = k & -k
        for side, via in enumerate((low, k - low)):
            part = pl.ds(side * (tokens // 2), tokens // 2)
            relays[k, side] = to_peer(
                via, og.at[k - via, part], og.at[k, part], r_send.at[k, side], r_recv.at[k, side]
            )
    for copy in og_copies.values():
        copy.start()
    early = [k for k in order if crossings(k) > 1] + [1]
    for k in early:
        oc_copies[k].start()

    fill_basis(band_ref, bh, bl, bt)

    for k in direct:
        og_copies[k].wait_recv()
    for copy in relays.values():
        copy.start()
    for k in order:
        if k not in early:
            oc_copies[k].start()
    for k in direct:
        forward[k].start()

    loads[0].wait()
    span = slabs * LANES
    row = lax.broadcasted_iota(jnp.int32, (span, LANES), 0)
    lane = lax.broadcasted_iota(jnp.int32, (span, LANES), 1)
    for a in range(slabs):
        perm[:, a * LANES : (a + 1) * LANES] = (row == slabs * lane + a).astype(F32).astype(BF16)
    for piece in range(depth // span):
        sorted_piece = dot(x[:, piece * span : (piece + 1) * span], perm[...]).astype(BF16)
        for a in range(slabs):
            xa[a * tokens : (a + 1) * tokens, piece * LANES : (piece + 1) * LANES] = sorted_piece[
                :, a * LANES : (a + 1) * LANES
            ]
    for k in relayed:
        relays[k, 0].wait_recv()
        relays[k, 1].wait_recv()
        forward[k].start()

    for load in loads[1:]:
        load.wait()
    tiles = range(width // LANES)
    first = dot(oc[0], og[0], ((0,), (0,)))
    for t in tiles:
        grad[t] = first[:, t * LANES : (t + 1) * LANES]
    even[0] = dot(oc[0], w[...])
    to_partner = {}
    for k in [1] + order:
        oc_copies[k].wait_recv()
        if k % 2 and k > 1:
            forward[k - 1].wait_recv()
        elif k == 1:
            og_copies[1].wait_recv()
        product = dot(oc[k], og[k], ((0,), (0,)))
        for t in tiles:
            grad[t] += product[:, t * LANES : (t + 1) * LANES]
        partial = dot(oc[k], w[...])
        if k % 2:
            odd[k // 2] = partial.astype(BF16)
            to_partner[k] = to_peer(1, odd.at[k // 2], pin.at[k // 2], p_send.at[k // 2], p_recv.at[k // 2])
            to_partner[k].start()
        else:
            even[k // 2] = partial

    v_copies = {}
    for h in range(n // 2 - 1, 0, -1):
        to_partner[2 * h + 1].wait_recv()
        pout[h] = (even[h] + pin[h].astype(F32)).astype(BF16)
        copy = to_peer(2 * h, pout.at[h], vin.at[h], v_send.at[h], v_recv.at[h])
        copy.start()
        v_copies[h] = copy

    wide, narrow = None, None
    for a in range(slabs):
        rows = [grad[t, pl.ds(a, groups, stride=slabs), :] for t in tiles]
        part = MOMENTUM_DECAY * mom[:, a * width : (a + 1) * width] + scaling * jnp.concatenate(rows, 1)
        mom[:, a * width : (a + 1) * width] = part
        hi, lo = split_hi_lo(part)
        both = dot(hi, bt[a * width : (a + 1) * width, :])
        rest = dot(lo, bt[a * width : (a + 1) * width, :bands])
        wide = both if wide is None else wide + both
        narrow = rest if narrow is None else narrow + rest
    total = wide[:, :bands] + (wide[:, bands:] + narrow)
    cz[rep] = total.astype(BF16)
    c_copies = [to_rep(d, cz.at[rep], cz.at[rep], c_send.at[d], c_recv.at[d]) for d in range(1, reps)]
    for c in c_copies:
        c.start()

    c_hi, c_lo = split_hi_lo(total)
    for a in range(slabs):
        cut = slice(a * width, (a + 1) * width)
        left[0, :, cut] = mom[:, cut] - dot3(c_hi, c_lo, bh[a], bl[a])

    for c in c_copies:
        c.wait_recv()
    shared = cz[0].astype(F32)
    for d in range(1, reps):
        shared = shared + cz[d].astype(F32)
    shared = shared / reps
    sg[me] = shared.astype(BF16)
    s_copies = [to_peer(k, sg.at[me], sg.at[me], s_send.at[k], s_recv.at[k]) for k in range(n - 1, 0, -1)]
    for s in s_copies:
        s.start()

    s_hi, s_lo = split_hi_lo(shared)
    for a in range(slabs):
        product = dot3(s_hi, s_lo, bh[a], bl[a])
        for t in tiles:
            upd[t, pl.ds(a, groups, stride=slabs), :] = product[:, t * LANES : (t + 1) * LANES]
    for t in tiles:
        cut = slice(t * LANES, (t + 1) * LANES)
        nw[:, cut] = rebuild_rows(w[:, cut], upd[t])

    to_partner[1].wait_recv()
    base = even[0] + pin[0].astype(F32)
    for h in range(1, n // 2):
        v_copies[h].wait_recv()
        base = base + vin[h].astype(F32)
    for s in s_copies:
        s.wait_recv()
    mixed = dot(xa[...], sg[...].reshape(n * groups, bands))
    mixed = jnp.concatenate([mixed[a * tokens : (a + 1) * tokens] for a in range(slabs)], 1)
    hi, lo = split_hi_lo(mixed)
    change = dot3(hi, lo, bh[...].reshape(slabs * bands, width), bl[...].reshape(slabs * bands, width))
    val[0] = ((base - LEARNING_RATE * change) * scaling).astype(BF16)

    for k in range(1, n):
        oc_copies[k].wait_send()
        if k % 2 and k > 1:
            forward[k - 1].wait_send()
        elif k in relayed:
            relays[k, 0].wait_send()
            relays[k, 1].wait_send()
        else:
            og_copies[k].wait_send()
        if k % 2:
            to_partner[k].wait_send()
    for copy in list(v_copies.values()) + c_copies + s_copies:
        copy.wait_send()


def store_kernel(left, nw, val, left_hbm, nw_hbm, val_hbm, sems):
    copies = [
        pltpu.make_async_copy(src, dst, sems.at[i])
        for i, (src, dst) in enumerate(((left, left_hbm), (nw, nw_hbm), (val, val_hbm)))
    ]
    for copy in copies:
        copy.start()
    for copy in copies:
        copy.wait()


def fused_shards(n, reps, inputs, out_grad, weight, momentum, band_index):
    tokens, depth = inputs.shape[1:]
    own_rows, width = weight.shape
    groups, group_len = momentum.shape[1:]
    slabs, bands = group_len // width, band_index.shape[0]
    half = n // 2
    dma = pltpu.SemaphoreType.DMA
    span = slabs * LANES
    anywhere = pl.BlockSpec(memory_space=pl.ANY)
    held = pl.pallas_call(
        functools.partial(kernel, n, reps),
        out_shape=(
            pltpu.VMEM(momentum.shape, F32),
            pltpu.VMEM(weight.shape, BF16),
            pltpu.VMEM(out_grad.shape, BF16),
        ),
        in_specs=[pl.BlockSpec(memory_space=pltpu.VMEM)] + [anywhere] * 4,
        out_specs=(pl.BlockSpec(memory_space=pltpu.VMEM),) * 3,
        scratch_shapes=[
            pltpu.VMEM((tokens, depth), BF16),
            pltpu.VMEM((n, tokens, own_rows), BF16),
            pltpu.VMEM((n, tokens, width), BF16),
            pltpu.VMEM((own_rows, width), BF16),
            pltpu.VMEM((groups, group_len), F32),
            pltpu.VMEM((slabs, bands, width), BF16),
            pltpu.VMEM((slabs, bands, width), BF16),
            pltpu.VMEM((group_len, 2 * bands), BF16),
            pltpu.VMEM((span, span), BF16),
            pltpu.VMEM((slabs * tokens, depth // slabs), BF16),
            pltpu.VMEM((width // LANES, own_rows, LANES), F32),
            pltpu.VMEM((width // LANES, own_rows, LANES), F32),
            pltpu.VMEM((half, tokens, width), BF16),
            pltpu.VMEM((half, tokens, width), F32),
            pltpu.VMEM((half, tokens, width), BF16),
            pltpu.VMEM((half, tokens, width), BF16),
            pltpu.VMEM((half, tokens, width), BF16),
            pltpu.VMEM((reps, groups, bands), BF16),
            pltpu.VMEM((n, groups, bands), BF16),
            dma((5,)),
            dma((n,)), dma((n,)), dma((n,)), dma((n,)), dma((n, 2)), dma((n, 2)),
            dma((half,)), dma((half,)), dma((half,)), dma((half,)),
            dma((reps,)), dma((reps,)), dma((n,)), dma((n,)),
        ],
        compiler_params=pltpu.CompilerParams(collective_id=0, has_side_effects=True),
    )(band_index.reshape(1, -1), inputs, out_grad, weight, momentum)
    return pl.pallas_call(
        store_kernel,
        out_shape=tuple(jax.ShapeDtypeStruct(a.shape, a.dtype) for a in held),
        in_specs=[anywhere] * 3,
        out_specs=(anywhere,) * 3,
        scratch_shapes=[dma((3,))],
        compiler_params=pltpu.CompilerParams(vmem_limit_bytes=1 << 20),
    )(*held)


def fits_kernel(n, inputs, weight, momentum, band_index):
    tokens, depth = inputs.shape[1:]
    own_rows, width = weight.shape
    groups, group_len = momentum.shape[1:]
    return (
        n > 1
        and n & (n - 1) == 0
        and group_len & (group_len - 1) == 0
        and tokens % 32 == 0
        and own_rows % LANES == 0
        and width % LANES == 0
        and groups % 16 == 0
        and group_len % width == 0
        and group_len // LANES <= LANES
        and depth % (group_len // width * LANES) == 0
        and band_index.shape[0] % LANES == 0
    )


def program(n, reps, inputs, out_grad, weight, momentum, band_index):
    if fits_kernel(n, inputs, weight, momentum, band_index):
        return fused_shards(n, reps, inputs, out_grad, weight, momentum, band_index)
    return shards(inputs, out_grad, weight, momentum, band_index)


def solution(mesh):
    placed = (
        P("rep", "fsdp", None),
        P("rep", "fsdp", None),
        P("fsdp", None),
        P("rep", "fsdp", None),
        P(),
    )
    return jax.shard_map(
        functools.partial(program, mesh.shape["fsdp"], mesh.shape["rep"]),
        mesh=mesh,
        in_specs=placed,
        out_specs=(P("rep", "fsdp", None), P("fsdp", None), P("rep", "fsdp", None)),
        check_vma=False,
    )
```

profile of v0, /device:TPU:0, one launch (start us, length us, event | category | flops | bytes accessed | tf_op | source)
XLA Modules:
  0.0 37.6 jit_solution(13199146799306955150)
XLA Ops:
  0.6 35.7 %shard_map.76 = (f32[1,64,4096]{2,1,0:T(8,128)S(1)}, bf16[512,512]{1,0:T(8,128)(2,1)S(1)}, bf16[1,128,512]{2,1,0:T(8,128)(2,1)S(1)}) custom-call(s32[1,128]{1,0:T(1,128)} %bitcast.1, bf16[1,128,4096]{2,1,0:T(8,128)(2,1)} %x_hbm.1, bf16[1,128,512]{2,1,0:T(8,128)(2,1)} %og_hbm.1, bf16[512,512]{1,0:T(8,128)(2,1)} %w_hbm.1, f32[1,64,4096]{2,1,0:T(8,128)} %mom_hbm.1), custom_call_target="tpu_custom_call" | custom-call | tf_op jit(solution)/shard_map/pallas_call | solution.py:344
  36.4 1.2 %shard_map.77 = (f32[1,64,4096]{2,1,0:T(8,128)}, bf16[512,512]{1,0:T(8,128)(2,1)}, bf16[1,128,512]{2,1,0:T(8,128)(2,1)}) custom-call(f32[1,64,4096]{2,1,0:T(8,128)S(1)} %get-tuple-element.6.left, bf16[512,512]{1,0:T(8,128)(2,1)S(1)} %get-tuple-element.7.nw, bf16[1,128,512]{2,1,0:T(8,128)(2,1)S(1)} %get-tuple-element.8.val), custom_call_target="tpu_custom_call" | custom-call | tf_op jit(solution)/shard_map/pallas_call | solution.py:380
where the time goes:
time: 37.7 us; the launch traced here: 37.6 us
  Pallas kernels  36.9 us (98%)
  between operations  0.64 us (2%)
    pallas_call x1, Pallas kernels, fused_shards(): pl.pallas_call(functools.partial(kernel, n, reps), out_shape=(pltpu.VMEM(...  35.7 us
    pallas_call x1, Pallas kernels, fused_shards(): pl.pallas_call(store_kernel, out_shape=tuple((jax.ShapeDtypeStruct(a.shap...  1.2 us

commit v1 on v0

v1 whole, which is shorter than its diff:
```python
import functools
import math

import jax
import jax.numpy as jnp
from jax import lax
from jax.experimental import pallas as pl
from jax.experimental.pallas import tpu as pltpu
from jax.sharding import PartitionSpec as P

MOMENTUM_DECAY = 0.9
LEARNING_RATE = 4.0


def dct_rows(band_index, length):
    positions = lax.iota(jnp.int32, length)
    phase_int = (2 * positions[None, :] + 1) * band_index[:, None] % (4 * length)
    angles = phase_int.astype(jnp.float32) * (math.pi / (2 * length))
    row_scale = jnp.where(band_index == 0, math.sqrt(1.0 / length), math.sqrt(2.0 / length)).astype(
        jnp.float32
    )
    return row_scale[:, None] * jnp.cos(angles)


def rebuild_rows(old_rows, update_rows):
    return (old_rows.astype(jnp.float32) - LEARNING_RATE * update_rows).astype(jnp.bfloat16)


def shards(inputs, out_grad, weight, momentum, band_index):
    tok_inputs = inputs[0]
    upstream = out_grad[0]
    own_rows = weight.shape[0]
    width_out = weight.shape[1]
    group_len = momentum.shape[2]
    scaling = 1.0 / math.sqrt(tok_inputs.shape[1])
    highest = lax.Precision.HIGHEST
    own_columns = lax.all_to_all(tok_inputs, "fsdp", split_axis=1, concat_axis=0, tiled=True)
    gradient = (
        lax.dot_general(
            own_columns,
            lax.all_gather(upstream, "fsdp", axis=0, tiled=True),
            (((0,), (0,)), ((), ())),
            preferred_element_type=jnp.float32,
        )
        * scaling
    )
    moment = MOMENTUM_DECAY * momentum[0] + gradient.reshape(-1, group_len)
    dct_basis = dct_rows(band_index, group_len)
    coeffs = jnp.dot(moment, dct_basis.T, precision=highest)
    leftover = (moment - jnp.dot(coeffs, dct_basis, precision=highest))[None]
    shared = lax.psum(coeffs, "rep") / lax.axis_size("rep")
    own_update = jnp.dot(shared, dct_basis, precision=highest).reshape(own_rows, width_out)
    new_weight = rebuild_rows(weight, own_update)
    running = jnp.dot(
        tok_inputs,
        lax.all_gather(new_weight, "fsdp", axis=0, tiled=True),
        preferred_element_type=jnp.float32,
    )
    values = (running * scaling).astype(jnp.bfloat16)[None]
    return (leftover, new_weight, values)


LANES = 128
F32, BF16 = jnp.float32, jnp.bfloat16


def split_hi_lo(x):
    hi = x.astype(BF16)
    return hi, (x - hi.astype(F32)).astype(BF16)


def dot(a, b, dims=((1,), (0,))):
    return lax.dot_general(a, b, (dims, ((), ())), preferred_element_type=F32)


def dot3(a_hi, a_lo, b_hi, b_lo, dims=((1,), (0,))):
    return dot(a_hi, b_hi, dims) + dot(a_hi, b_lo, dims) + dot(a_lo, b_hi, dims)


def fill_basis(band_ref, bh, bl, bt, between):
    slabs, bands, width = bh.shape
    length = slabs * width
    period = 4 * length
    freq = jnp.broadcast_to(band_ref[...].astype(F32), (LANES, bands)).T.astype(jnp.int32)
    lane = lax.broadcasted_iota(jnp.int32, (bands, LANES), 1)
    row_scale = jnp.where(freq == 0, math.sqrt(1.0 / length), math.sqrt(2.0 / length)).astype(F32)

    def angle(steps):
        centred = ((steps * freq + period // 2) & (period - 1)) - period // 2
        return centred.astype(F32) * (math.pi / (2 * length))

    fine, coarse = angle(2 * lane + 1), angle(2 * LANES * lane)
    cos_fine, sin_fine = row_scale * jnp.cos(fine), row_scale * jnp.sin(fine)
    cos_coarse, sin_coarse = jnp.cos(coarse), jnp.sin(coarse)
    between()
    for at in range(length // LANES):
        tile = cos_coarse[:, at : at + 1] * cos_fine - sin_coarse[:, at : at + 1] * sin_fine
        hi, lo = split_hi_lo(tile)
        a, col = divmod(at * LANES, width)
        bh[a, :, col : col + LANES] = hi
        bl[a, :, col : col + LANES] = lo
        hi, lo = split_hi_lo(tile.T)
        bt[at * LANES : (at + 1) * LANES, :bands] = hi
        bt[at * LANES : (at + 1) * LANES, bands:] = lo


CORE, SIDES, DIAGONAL = 1, (2, 4), 6


def kernel(
    n, reps, band_hbm, x_hbm, og_hbm, w_hbm, mom_hbm, left, nw, val,
    band, x, oc, og, w, mom, bh, bl, bt, perm, xa, zc, grad, upd, even, odd, pin, vout, vin, hout, hin,
    cl, cpo, cpi, cro, cri, cz, sg,
    load_sem, x_send, x_recv, og_send, og_recv, p_send, p_recv, v_send, h_recv, v_recv, c_send, c_recv,
    far_fsdp, far_rep,
):
    me, rep = lax.axis_index("fsdp"), lax.axis_index("rep")
    tokens, depth = x.shape
    own_rows, width = w.shape
    slabs, bands, _ = bh.shape
    groups = mom.shape[0]
    half_tokens = tokens // 2
    scaling = 1.0 / math.sqrt(depth)
    bits = n.bit_length() - 1

    def peer(k):
        return sum((((me // 2**b) % 2 + (k >> b) % 2) % 2) * 2**b for b in range(bits))

    def columns(which):
        return pl.ds(pl.multiple_of(which * own_rows, LANES), own_rows)

    def to_peer(k, src, dst, send, recv):
        return pltpu.make_async_remote_copy(
            src_ref=src, dst_ref=dst, send_sem=send, recv_sem=recv,
            device_id={"fsdp": peer(k)}, device_id_type=pl.DeviceIdType.MESH,
        )

    def to_rep(d, src, dst, send, recv):
        return pltpu.make_async_remote_copy(
            src_ref=src, dst_ref=dst, send_sem=send, recv_sem=recv,
            device_id={"rep": lax.rem(rep + d, reps)}, device_id_type=pl.DeviceIdType.MESH,
        )

    def wait_bytes(like, sem):
        pltpu.make_async_copy(like, like, sem).wait()

    def signal_peer(sem, k):
        pl.semaphore_signal(sem, inc=1, device_id={"fsdp": peer(k)}, device_id_type=pl.DeviceIdType.MESH)

    def signal_next_reps(sem):
        for there, step in ((rep > 0, -1), (rep < reps - 1, 1)):

            @pl.when(there)
            def _():
                pl.semaphore_signal(
                    sem, inc=1, device_id={"rep": rep + step}, device_id_type=pl.DeviceIdType.MESH
                )

    next_reps = (rep > 0).astype(jnp.int32) + (rep < reps - 1).astype(jnp.int32)
    barrier = pltpu.get_barrier_semaphore()
    near = [CORE] + [k + c for k in SIDES for c in (0, CORE)]
    signal_next_reps(barrier)
    for k in near:
        signal_peer(barrier, k)
    loads = [
        pltpu.make_async_copy(src, dst, load_sem.at[i])
        for i, (src, dst) in enumerate(
            (
                (band_hbm, band),
                (x_hbm.at[0], x),
                (og_hbm.at[0], og.at[0]),
                (w_hbm, w),
                (mom_hbm.at[0], mom),
                (x_hbm.at[0, :, columns(me)], oc.at[0]),
            )
        )
    ]
    for load in loads:
        load.start()
    pl.semaphore_wait(barrier, len(near) + next_reps)

    signal_peer(far_fsdp, SIDES[0])
    if reps > 2:
        signal_next_reps(far_rep.at[0])
    og_copies = {k: to_peer(k, og_hbm.at[0], og.at[k], og_send, og_recv.at[k]) for k in (*SIDES, CORE)}
    x_copies = {
        k: to_peer(k, x_hbm.at[0, :, columns(peer(k))], oc.at[k], x_send, x_recv.at[k]) for k in range(1, n)
    }
    forward = {
        k: to_peer(CORE, og.at[k], og.at[k + CORE], og_send, og_recv.at[k + CORE])
        for k in (*SIDES, DIAGONAL)
    }
    parts = [pl.ds(side * half_tokens, half_tokens) for side in range(2)]
    relays = [
        to_peer(
            SIDES[side], og.at[SIDES[1 - side], parts[side]], og.at[DIAGONAL, parts[side]],
            og_send, og_recv.at[DIAGONAL],
        )
        for side in range(2)
    ]
    for copy in og_copies.values():
        copy.start()
    x_copies[CORE].start()

    def reach_diagonal():
        pl.semaphore_wait(far_fsdp, 1)
        x_copies[DIAGONAL].start()

    loads[0].wait()
    fill_basis(band, bh, bl, bt, reach_diagonal)

    for k in SIDES:
        og_copies[k].wait_recv()
    for copy in relays:
        copy.start()
    x_copies[DIAGONAL + CORE].start()
    for k in SIDES:
        forward[k].start()

    loads[1].wait()
    span = slabs * LANES
    row = lax.broadcasted_iota(jnp.int32, (span, LANES), 0)
    lane = lax.broadcasted_iota(jnp.int32, (span, LANES), 1)
    for a in range(slabs):
        perm[:, a * LANES : (a + 1) * LANES] = (row == slabs * lane + a).astype(F32).astype(BF16)
    for piece in range(depth // span):
        sorted_piece = dot(x[:, piece * span : (piece + 1) * span], perm[...]).astype(BF16)
        for a in range(slabs):
            xa[a * tokens : (a + 1) * tokens, piece * LANES : (piece + 1) * LANES] = sorted_piece[
                :, a * LANES : (a + 1) * LANES
            ]

    loads[2].wait()
    for a in range(slabs):
        both = dot(og[0], bt[a * width : (a + 1) * width, :])
        hi, lo = split_hi_lo(both[:, :bands] + both[:, bands:])
        zc[a * tokens : (a + 1) * tokens, :bands] = hi
        zc[a * tokens : (a + 1) * tokens, bands:] = lo
    both = dot(xa[...], zc[...], ((0,), (0,)))
    cl[...] = (scaling * (both[:, :bands] + both[:, bands:])).reshape(n, groups, bands)
    for h in range(n // 2):
        cpo[h] = cl[peer(2 * h + CORE)].astype(BF16)
    pair_copy = to_peer(CORE, cpo, cpi, c_send.at[0], c_recv.at[0])
    pair_copy.start()

    def coefficients(slab_of):
        wide, narrow = None, None
        for a in range(slabs):
            hi, lo = split_hi_lo(slab_of(a))
            both = dot(hi, bt[a * width : (a + 1) * width, :])
            rest = dot(lo, bt[a * width : (a + 1) * width, :bands])
            wide = both if wide is None else wide + both
            narrow = rest if narrow is None else narrow + rest
        return wide[:, :bands] + (wide[:, bands:] + narrow)

    for load in loads[3:]:
        load.wait()
    from_momentum = coefficients(lambda a: MOMENTUM_DECAY * mom[:, a * width : (a + 1) * width])
    pair_copy.wait_recv()
    chip_copies = []
    for h in range(1, n // 2):
        cro[h] = (cl[peer(2 * h)] + cpi[h].astype(F32)).astype(BF16)
        chip_copies.append(to_peer(2 * h, cro.at[h], cri.at[h], c_send.at[1], c_recv.at[1]))
        chip_copies[-1].start()
    for k in (*SIDES, *(k + CORE for k in SIDES)):
        x_copies[k].start()
    own_sum = from_momentum + (cl[me] + cpi[0].astype(F32))
    if reps > 2:
        for at in range(reps - 3):
            pl.semaphore_wait(far_rep.at[at], next_reps)
            signal_next_reps(far_rep.at[at + 1])

    tiles = range(width // LANES)
    first = dot(oc[0], og[0], ((0,), (0,)))
    for t in tiles:
        grad[t] = first[:, t * LANES : (t + 1) * LANES]
    even[0] = dot(oc[0], w[...])
    to_partner = {}

    def take(k):
        x_copies[k].wait_recv()
        partial = dot(oc[k], w[...])
        if k % 2:
            odd[k // 2] = partial.astype(BF16)
            to_partner[k] = to_peer(CORE, odd.at[k // 2], pin.at[k // 2], p_send, p_recv.at[k // 2])
            to_partner[k].start()
        else:
            even[k // 2] = partial
        if k == CORE:
            og_copies[CORE].wait_recv()
        elif k % 2:
            forward[k - CORE].wait_recv()
        product = dot(oc[k], og[k], ((0,), (0,)))
        for t in tiles:
            grad[t] += product[:, t * LANES : (t + 1) * LANES]

    take(CORE)
    wait_bytes(og.at[DIAGONAL], og_recv.at[DIAGONAL])
    forward[DIAGONAL].start()
    take(DIAGONAL)
    take(DIAGONAL + CORE)

    wait_bytes(cri.at[1 : n // 2], c_recv.at[1])
    for h in range(1, n // 2):
        own_sum = own_sum + cri[h].astype(F32)
    cz[rep] = own_sum.astype(BF16)
    if reps > 2:
        pl.semaphore_wait(far_rep.at[reps - 3], next_reps)
    for d in range(1, reps):
        to_rep(d, cz.at[rep], cz.at[rep], c_send.at[2], c_recv.at[2]).start()

    to_partner[DIAGONAL + CORE].wait_recv()
    across = even[DIAGONAL // 2] + pin[DIAGONAL // 2].astype(F32)
    halves = []
    for side, k in enumerate(SIDES):
        hout[side] = across[side * half_tokens : (side + 1) * half_tokens].astype(BF16)
        halves.append(to_peer(k, hout.at[side], hin.at[side], v_send, h_recv.at[side]))
        halves[-1].start()
    take(SIDES[0])
    take(SIDES[1])

    wait_bytes(cz.at[: reps - 1], c_recv.at[2])
    shared = cz[0].astype(F32)
    for d in range(1, reps):
        shared = shared + cz[d].astype(F32)
    shared = shared / reps
    sg[me] = shared.astype(BF16)
    for k in (*SIDES, DIAGONAL):
        to_peer(k, sg.at[me], sg.at[me], c_send.at[3], c_recv.at[3]).start()
    to_peer(CORE, sg.at[me], sg.at[me], c_send.at[3], c_recv.at[4]).start()
    take(SIDES[0] + CORE)
    take(SIDES[1] + CORE)

    v_copies = []
    for side, k in enumerate(SIDES):
        to_partner[k + CORE].wait_recv()
        halves[1 - side].wait_recv()
        both = even[k // 2] + pin[k // 2].astype(F32)
        cut = slice((1 - side) * half_tokens, (2 - side) * half_tokens)
        same = slice(side * half_tokens, (side + 1) * half_tokens)
        vout[side, same] = both[same].astype(BF16)
        vout[side, cut] = (both[cut] + hin[1 - side].astype(F32)).astype(BF16)
        v_copies.append(to_peer(k, vout.at[side], vin.at[side], v_send, v_recv.at[side]))
        v_copies[-1].start()

    wait_bytes(sg.at[:3], c_recv.at[3])
    for k in (*SIDES, DIAGONAL):
        to_peer(CORE, sg.at[peer(k)], sg.at[peer(k)], c_send.at[3], c_recv.at[4]).start()

    def gradient_slab(a):
        rows = [grad[t, pl.ds(a, groups, stride=slabs), :] for t in tiles]
        return scaling * jnp.concatenate(rows, 1)

    def keep_moment(a):
        part = gradient_slab(a)
        cut = slice(a * width, (a + 1) * width)
        mom[:, cut] = MOMENTUM_DECAY * mom[:, cut] + part
        return part

    c_hi, c_lo = split_hi_lo(from_momentum + coefficients(keep_moment))
    for a in range(slabs):
        cut = slice(a * width, (a + 1) * width)
        left[0, :, cut] = mom[:, cut] - dot3(c_hi, c_lo, bh[a], bl[a])

    s_hi, s_lo = split_hi_lo(shared)
    for a in range(slabs):
        product = dot3(s_hi, s_lo, bh[a], bl[a])
        for t in tiles:
            upd[t, pl.ds(a, groups, stride=slabs), :] = product[:, t * LANES : (t + 1) * LANES]
    for t in tiles:
        cut = slice(t * LANES, (t + 1) * LANES)
        nw[:, cut] = rebuild_rows(w[:, cut], upd[t])

    wait_bytes(sg.at[:4], c_recv.at[4])
    mixed = dot(xa[...], sg[...].reshape(n * groups, bands))
    mixed = jnp.concatenate([mixed[a * tokens : (a + 1) * tokens] for a in range(slabs)], 1)
    hi, lo = split_hi_lo(mixed)
    change = dot3(hi, lo, bh[...].reshape(slabs * bands, width), bl[...].reshape(slabs * bands, width))
    to_partner[CORE].wait_recv()
    base = even[0] + pin[0].astype(F32) - LEARNING_RATE * change
    for copy in v_copies:
        copy.wait_recv()
    for side in range(2):
        base = base + vin[side].astype(F32)
    val[0] = (base * scaling).astype(BF16)

    wait_bytes(oc.at[1:], x_send)
    wait_bytes(og.at[1:], og_send)
    wait_bytes(odd, p_send)
    wait_bytes(odd.at[:3], v_send)
    wait_bytes(cpo, c_send.at[0])
    wait_bytes(cri.at[1:], c_send.at[1])
    wait_bytes(cz.at[: reps - 1], c_send.at[2])
    wait_bytes(sg.at[:7], c_send.at[3])


def store_kernel(left, nw, val, left_hbm, nw_hbm, val_hbm, sems):
    copies = [
        pltpu.make_async_copy(src, dst, sems.at[i])
        for i, (src, dst) in enumerate(((left, left_hbm), (nw, nw_hbm), (val, val_hbm)))
    ]
    for copy in copies:
        copy.start()
    for copy in copies:
        copy.wait()


def fused_shards(n, reps, inputs, out_grad, weight, momentum, band_index):
    tokens, depth = inputs.shape[1:]
    own_rows, width = weight.shape
    groups, group_len = momentum.shape[1:]
    slabs, bands = group_len // width, band_index.shape[0]
    half = n // 2
    dma, regular = pltpu.SemaphoreType.DMA, pltpu.SemaphoreType.REGULAR
    span = slabs * LANES
    anywhere = pl.BlockSpec(memory_space=pl.ANY)
    held = pl.pallas_call(
        functools.partial(kernel, n, reps),
        out_shape=(
            pltpu.VMEM(momentum.shape, F32),
            pltpu.VMEM(weight.shape, BF16),
            pltpu.VMEM(out_grad.shape, BF16),
        ),
        in_specs=[anywhere] * 5,
        out_specs=(pl.BlockSpec(memory_space=pltpu.VMEM),) * 3,
        scratch_shapes=[
            pltpu.VMEM((1, bands), jnp.int32),
            pltpu.VMEM((tokens, depth), BF16),
            pltpu.VMEM((n, tokens, own_rows), BF16),
            pltpu.VMEM((n, tokens, width), BF16),
            pltpu.VMEM((own_rows, width), BF16),
            pltpu.VMEM((groups, group_len), F32),
            pltpu.VMEM((slabs, bands, width), BF16),
            pltpu.VMEM((slabs, bands, width), BF16),
            pltpu.VMEM((group_len, 2 * bands), BF16),
            pltpu.VMEM((span, span), BF16),
            pltpu.VMEM((slabs * tokens, depth // slabs), BF16),
            pltpu.VMEM((slabs * tokens, 2 * bands), BF16),
            pltpu.VMEM((width // LANES, own_rows, LANES), F32),
            pltpu.VMEM((width // LANES, own_rows, LANES), F32),
            pltpu.VMEM((half, tokens, width), F32),
            pltpu.VMEM((half, tokens, width), BF16),
            pltpu.VMEM((half, tokens, width), BF16),
            pltpu.VMEM((2, tokens, width), BF16),
            pltpu.VMEM((2, tokens, width), BF16),
            pltpu.VMEM((2, tokens // 2, width), BF16),
            pltpu.VMEM((2, tokens // 2, width), BF16),
            pltpu.VMEM((n, groups, bands), F32),
            pltpu.VMEM((half, groups, bands), BF16),
            pltpu.VMEM((half, groups, bands), BF16),
            pltpu.VMEM((half, groups, bands), BF16),
            pltpu.VMEM((half, groups, bands), BF16),
            pltpu.VMEM((reps, groups, bands), BF16),
            pltpu.VMEM((n, groups, bands), BF16),
            dma((6,)),
            dma, dma((n,)), dma, dma((n,)), dma, dma((half,)), dma, dma((2,)), dma((2,)),
            dma((4,)), dma((5,)),
            regular, regular((max(reps - 2, 1),)),
        ],
        compiler_params=pltpu.CompilerParams(collective_id=0, has_side_effects=True),
    )(band_index.reshape(1, -1), inputs, out_grad, weight, momentum)
    return pl.pallas_call(
        store_kernel,
        out_shape=tuple(jax.ShapeDtypeStruct(a.shape, a.dtype) for a in held),
        in_specs=[anywhere] * 3,
        out_specs=(anywhere,) * 3,
        scratch_shapes=[dma((3,))],
        compiler_params=pltpu.CompilerParams(vmem_limit_bytes=1 << 20),
    )(*held)


def fits_kernel(n, reps, inputs, weight, momentum, band_index):
    tokens, depth = inputs.shape[1:]
    own_rows, width = weight.shape
    groups, group_len = momentum.shape[1:]
    return (
        n == CORE + DIAGONAL + 1
        and reps > 1
        and group_len & (group_len - 1) == 0
        and tokens % 32 == 0
        and own_rows % LANES == 0
        and width % LANES == 0
        and groups % 16 == 0
        and group_len % width == 0
        and group_len // LANES <= LANES
        and depth % (group_len // width * LANES) == 0
        and n * groups * (group_len // width) == depth
        and band_index.shape[0] % LANES == 0
    )


def program(n, reps, inputs, out_grad, weight, momentum, band_index):
    if fits_kernel(n, reps, inputs, weight, momentum, band_index):
        return fused_shards(n, reps, inputs, out_grad, weight, momentum, band_index)
    return shards(inputs, out_grad, weight, momentum, band_index)


def solution(mesh):
    placed = (
        P("rep", "fsdp", None),
        P("rep", "fsdp", None),
        P("fsdp", None),
        P("rep", "fsdp", None),
        P(),
    )
    return jax.shard_map(
        functools.partial(program, mesh.shape["fsdp"], mesh.shape["rep"]),
        mesh=mesh,
        in_specs=placed,
        out_specs=(P("rep", "fsdp", None), P("fsdp", None), P("rep", "fsdp", None)),
        check_vma=False,
    )
```

time: 37.7 us -> 31.7 us (0.84)
  Pallas kernels: 36.9 us -> 30.9 us
    pallas_call x1, Pallas kernels: 35.7 us -> 29.7 us  [fused_shards(): pl.pallas_call(functools.partial(kernel, n, reps), out_shape=(pltpu.VMEM(...]
where the time goes in v1:
time: 31.7 us; the launch traced here: 31.5 us
  Pallas kernels  30.9 us (97%)
  between operations  0.64 us (2%)
    pallas_call x1, Pallas kernels, fused_shards(): pl.pallas_call(functools.partial(kernel, n, reps), out_shape=(pltpu.VMEM(...  29.7 us
    pallas_call x1, Pallas kernels, fused_shards(): pl.pallas_call(store_kernel, out_shape=tuple((jax.ShapeDtypeStruct(a.shap...  1.2 us

profile of v1, /device:TPU:0, one launch (start us, length us, event | category | flops | bytes accessed | tf_op | source)
XLA Modules:
  0.0 31.5 jit_solution(982154096833555671)
XLA Ops:
  0.6 29.7 %shard_map.76 = (f32[1,64,4096]{2,1,0:T(8,128)S(1)}, bf16[512,512]{1,0:T(8,128)(2,1)S(1)}, bf16[1,128,512]{2,1,0:T(8,128)(2,1)S(1)}) custom-call(s32[1,128]{1,0:T(1,128)} %bitcast.1, bf16[1,128,4096]{2,1,0:T(8,128)(2,1)} %x_hbm.1, bf16[1,128,512]{2,1,0:T(8,128)(2,1)} %og_hbm.1, bf16[512,512]{1,0:T(8,128)(2,1)} %w_hbm.1, f32[1,64,4096]{2,1,0:T(8,128)} %mom_hbm.1), custom_call_target="tpu_custom_call" | custom-call | tf_op jit(solution)/shard_map/pallas_call | solution.py:417
  30.3 1.2 %shard_map.77 = (f32[1,64,4096]{2,1,0:T(8,128)}, bf16[512,512]{1,0:T(8,128)(2,1)}, bf16[1,128,512]{2,1,0:T(8,128)(2,1)}) custom-call(f32[1,64,4096]{2,1,0:T(8,128)S(1)} %get-tuple-element.6.left, bf16[512,512]{1,0:T(8,128)(2,1)S(1)} %get-tuple-element.7.nw, bf16[1,128,512]{2,1,0:T(8,128)(2,1)S(1)} %get-tuple-element.8.val), custom_call_target="tpu_custom_call" | custom-call | tf_op jit(solution)/shard_map/pallas_call | solution.py:462

commit v2 on v1

--- a/solution.py
+++ b/solution.py
@@ -73,12 +73,14 @@
     return lax.dot_general(a, b, (dims, ((), ())), preferred_element_type=F32)
 
 
-def dot3(a_hi, a_lo, b_hi, b_lo, dims=((1,), (0,))):
-    return dot(a_hi, b_hi, dims) + dot(a_hi, b_lo, dims) + dot(a_lo, b_hi, dims)
-
-
-def fill_basis(band_ref, bh, bl, bt, between):
-    slabs, bands, width = bh.shape
+def doubled(x):
+    hi, lo = split_hi_lo(x)
+    return jnp.concatenate([jnp.concatenate([part, part], 1) for part in (hi, lo)], 0)
+
+
+def fill_basis(band_ref, bw, bt, between):
+    slabs, bands, width = bw.shape
+    bands //= 2
     length = slabs * width
     period = 4 * length
     freq = jnp.broadcast_to(band_ref[...].astype(F32), (LANES, bands)).T.astype(jnp.int32)
@@ -97,8 +99,8 @@
         tile = cos_coarse[:, at : at + 1] * cos_fine - sin_coarse[:, at : at + 1] * sin_fine
         hi, lo = split_hi_lo(tile)
         a, col = divmod(at * LANES, width)
-        bh[a, :, col : col + LANES] = hi
-        bl[a, :, col : col + LANES] = lo
+        bw[a, :bands, col : col + LANES] = hi
+        bw[a, bands:, col : col + LANES] = lo
         hi, lo = split_hi_lo(tile.T)
         bt[at * LANES : (at + 1) * LANES, :bands] = hi
         bt[at * LANES : (at + 1) * LANES, bands:] = lo
@@ -109,15 +111,15 @@
 
 def kernel(
     n, reps, band_hbm, x_hbm, og_hbm, w_hbm, mom_hbm, left, nw, val,
-    band, x, oc, og, w, mom, bh, bl, bt, perm, xa, zc, grad, upd, even, odd, pin, vout, vin, hout, hin,
+    band, x, oc, og, w, mom, bw, bt, perm, xa, zc, grad, upd, even, odd, pin, vout, vin, hout, hin,
     cl, cpo, cpi, cro, cri, cz, sg,
-    load_sem, x_send, x_recv, og_send, og_recv, p_send, p_recv, v_send, h_recv, v_recv, c_send, c_recv,
-    far_fsdp, far_rep,
+    load_sem, x_send, x_recv, last_recv, og_send, og_recv, p_send, p_recv, v_send, h_recv, v_recv, c_send, c_recv,
+    side_entered, rep_round, all_entered,
 ):
     me, rep = lax.axis_index("fsdp"), lax.axis_index("rep")
     tokens, depth = x.shape
     own_rows, width = w.shape
-    slabs, bands, _ = bh.shape
+    slabs, bands = bw.shape[0], bw.shape[1] // 2
     groups = mom.shape[0]
     half_tokens = tokens // 2
     scaling = 1.0 / math.sqrt(depth)
@@ -147,16 +149,33 @@
     def signal_peer(sem, k):
         pl.semaphore_signal(sem, inc=1, device_id={"fsdp": peer(k)}, device_id_type=pl.DeviceIdType.MESH)
 
+    first = me == 0
+
     def signal_next_reps(sem):
         for there, step in ((rep > 0, -1), (rep < reps - 1, 1)):
 
-            @pl.when(there)
+            @pl.when(first & there)
             def _():
                 pl.semaphore_signal(
                     sem, inc=1, device_id={"rep": rep + step}, device_id_type=pl.DeviceIdType.MESH
                 )
 
     next_reps = (rep > 0).astype(jnp.int32) + (rep < reps - 1).astype(jnp.int32)
+
+    def pass_on(at):
+        @pl.when(first)
+        def _():
+            pl.semaphore_wait(rep_round.at[at], next_reps)
+
+        if at + 1 < reps - 1:
+            signal_next_reps(rep_round.at[at + 1])
+            return
+        for k in range(1, n):
+
+            @pl.when(first)
+            def _():
+                signal_peer(all_entered, k)
+
     barrier = pltpu.get_barrier_semaphore()
     near = [CORE] + [k + c for k in SIDES for c in (0, CORE)]
     signal_next_reps(barrier)
@@ -177,20 +196,27 @@
     ]
     for load in loads:
         load.start()
-    pl.semaphore_wait(barrier, len(near) + next_reps)
-
-    signal_peer(far_fsdp, SIDES[0])
-    if reps > 2:
-        signal_next_reps(far_rep.at[0])
+    pl.semaphore_wait(barrier, len(near) + jnp.where(first, next_reps, 0))
+
+    signal_peer(side_entered, SIDES[0])
     og_copies = {k: to_peer(k, og_hbm.at[0], og.at[k], og_send, og_recv.at[k]) for k in (*SIDES, CORE)}
     x_copies = {
-        k: to_peer(k, x_hbm.at[0, :, columns(peer(k))], oc.at[k], x_send, x_recv.at[k]) for k in range(1, n)
+        k: to_peer(k, x_hbm.at[0, :, columns(peer(k))], oc.at[k], x_send, x_recv.at[k])
+        for k in range(1, n)
+        if k not in SIDES
+    }
+    parts = [pl.ds(side * half_tokens, half_tokens) for side in range(2)]
+    last_copies = {
+        (k, part): to_peer(
+            k, x_hbm.at[0, parts[part], columns(peer(k))], oc.at[k, parts[part]], x_send, last_recv.at[i, part]
+        )
+        for i, k in enumerate(SIDES)
+        for part in range(2)
     }
     forward = {
         k: to_peer(CORE, og.at[k], og.at[k + CORE], og_send, og_recv.at[k + CORE])
         for k in (*SIDES, DIAGONAL)
     }
-    parts = [pl.ds(side * half_tokens, half_tokens) for side in range(2)]
     relays = [
         to_peer(
             SIDES[side], og.at[SIDES[1 - side], parts[side]], og.at[DIAGONAL, parts[side]],
@@ -203,20 +229,14 @@
     x_copies[CORE].start()
 
     def reach_diagonal():
-        pl.semaphore_wait(far_fsdp, 1)
+        pl.semaphore_wait(side_entered, 1)
         x_copies[DIAGONAL].start()
+        signal_next_reps(rep_round.at[0])
 
     loads[0].wait()
-    fill_basis(band, bh, bl, bt, reach_diagonal)
-
-    for k in SIDES:
-        og_copies[k].wait_recv()
-    for copy in relays:
-        copy.start()
-    x_copies[DIAGONAL + CORE].start()
-    for k in SIDES:
-        forward[k].start()
-
+    fill_basis(band, bw, bt, reach_diagonal)
+
+    pass_on(0)
     loads[1].wait()
     span = slabs * LANES
     row = lax.broadcasted_iota(jnp.int32, (span, LANES), 0)
@@ -243,41 +263,37 @@
     pair_copy = to_peer(CORE, cpo, cpi, c_send.at[0], c_recv.at[0])
     pair_copy.start()
 
+    pass_on(1)
+    for k in SIDES:
+        og_copies[k].wait_recv()
+    for copy in relays:
+        copy.start()
+    for k in SIDES:
+        forward[k].start()
+
     def coefficients(slab_of):
-        wide, narrow = None, None
+        both = None
         for a in range(slabs):
-            hi, lo = split_hi_lo(slab_of(a))
-            both = dot(hi, bt[a * width : (a + 1) * width, :])
-            rest = dot(lo, bt[a * width : (a + 1) * width, :bands])
-            wide = both if wide is None else wide + both
-            narrow = rest if narrow is None else narrow + rest
-        return wide[:, :bands] + (wide[:, bands:] + narrow)
+            stacked = jnp.concatenate(split_hi_lo(slab_of(a)), 0)
+            product = dot(stacked, bt[a * width : (a + 1) * width, :])
+            both = product if both is None else both + product
+        both = both[:, :bands] + both[:, bands:]
+        return both[:groups] + both[groups:]
+
+    def expand(stacked, a):
+        both = dot(stacked, bw[a])
+        return both[:groups] + both[groups:]
 
     for load in loads[3:]:
         load.wait()
-    from_momentum = coefficients(lambda a: MOMENTUM_DECAY * mom[:, a * width : (a + 1) * width])
-    pair_copy.wait_recv()
-    chip_copies = []
-    for h in range(1, n // 2):
-        cro[h] = (cl[peer(2 * h)] + cpi[h].astype(F32)).astype(BF16)
-        chip_copies.append(to_peer(2 * h, cro.at[h], cri.at[h], c_send.at[1], c_recv.at[1]))
-        chip_copies[-1].start()
-    for k in (*SIDES, *(k + CORE for k in SIDES)):
-        x_copies[k].start()
-    own_sum = from_momentum + (cl[me] + cpi[0].astype(F32))
-    if reps > 2:
-        for at in range(reps - 3):
-            pl.semaphore_wait(far_rep.at[at], next_reps)
-            signal_next_reps(far_rep.at[at + 1])
-
     tiles = range(width // LANES)
-    first = dot(oc[0], og[0], ((0,), (0,)))
+    product = dot(oc[0], og[0], ((0,), (0,)))
     for t in tiles:
-        grad[t] = first[:, t * LANES : (t + 1) * LANES]
+        grad[t] = product[:, t * LANES : (t + 1) * LANES]
     even[0] = dot(oc[0], w[...])
     to_partner = {}
 
-    def take(k):
+    def take_values(k):
         x_copies[k].wait_recv()
         partial = dot(oc[k], w[...])
         if k % 2:
@@ -286,6 +302,8 @@
             to_partner[k].start()
         else:
             even[k // 2] = partial
+
+    def take_gradient(k):
         if k == CORE:
             og_copies[CORE].wait_recv()
         elif k % 2:
@@ -294,21 +312,40 @@
         for t in tiles:
             grad[t] += product[:, t * LANES : (t + 1) * LANES]
 
+    def take(k):
+        take_values(k)
+        take_gradient(k)
+
     take(CORE)
-    wait_bytes(og.at[DIAGONAL], og_recv.at[DIAGONAL])
-    forward[DIAGONAL].start()
-    take(DIAGONAL)
-    take(DIAGONAL + CORE)
-
+    pair_copy.wait_recv()
+    for h in range(1, n // 2):
+        cro[h] = (cl[peer(2 * h)] + cpi[h].astype(F32)).astype(BF16)
+        to_peer(2 * h, cro.at[h], cri.at[h], c_send.at[1], c_recv.at[1]).start()
+    from_momentum = coefficients(lambda a: MOMENTUM_DECAY * mom[:, a * width : (a + 1) * width])
+    own_sum = from_momentum + (cl[me] + cpi[0].astype(F32))
+    for k in (DIAGONAL + CORE, *(k + CORE for k in SIDES)):
+        x_copies[k].start()
+    for at in range(2, reps - 1):
+        pass_on(at)
+    take_values(DIAGONAL)
     wait_bytes(cri.at[1 : n // 2], c_recv.at[1])
     for h in range(1, n // 2):
         own_sum = own_sum + cri[h].astype(F32)
     cz[rep] = own_sum.astype(BF16)
-    if reps > 2:
-        pl.semaphore_wait(far_rep.at[reps - 3], next_reps)
+
+    @pl.when(jnp.logical_not(first))
+    def _():
+        pl.semaphore_wait(all_entered, 1)
+
     for d in range(1, reps):
         to_rep(d, cz.at[rep], cz.at[rep], c_send.at[2], c_recv.at[2]).start()
 
+    wait_bytes(og.at[DIAGONAL], og_recv.at[DIAGONAL])
+    forward[DIAGONAL].start()
+    take_gradient(DIAGONAL)
+    for k in SIDES:
+        last_copies[k, 0].start()
+    take(DIAGONAL + CORE)
     to_partner[DIAGONAL + CORE].wait_recv()
     across = even[DIAGONAL // 2] + pin[DIAGONAL // 2].astype(F32)
     halves = []
@@ -316,8 +353,10 @@
         hout[side] = across[side * half_tokens : (side + 1) * half_tokens].astype(BF16)
         halves.append(to_peer(k, hout.at[side], hin.at[side], v_send, h_recv.at[side]))
         halves[-1].start()
-    take(SIDES[0])
-    take(SIDES[1])
+    for k in SIDES:
+        last_copies[k, 1].start()
+    take(SIDES[0] + CORE)
+    take(SIDES[1] + CORE)
 
     wait_bytes(cz.at[: reps - 1], c_recv.at[2])
     shared = cz[0].astype(F32)
@@ -328,24 +367,37 @@
     for k in (*SIDES, DIAGONAL):
         to_peer(k, sg.at[me], sg.at[me], c_send.at[3], c_recv.at[3]).start()
     to_peer(CORE, sg.at[me], sg.at[me], c_send.at[3], c_recv.at[4]).start()
-    take(SIDES[0] + CORE)
-    take(SIDES[1] + CORE)
+    agreed = doubled(shared)
+    for a in range(slabs):
+        product = expand(agreed, a)
+        for t in tiles:
+            upd[t, pl.ds(a, groups, stride=slabs), :] = product[:, t * LANES : (t + 1) * LANES]
+    for t in tiles:
+        cut = slice(t * LANES, (t + 1) * LANES)
+        nw[:, cut] = rebuild_rows(w[:, cut], upd[t])
 
     v_copies = []
-    for side, k in enumerate(SIDES):
-        to_partner[k + CORE].wait_recv()
-        halves[1 - side].wait_recv()
-        both = even[k // 2] + pin[k // 2].astype(F32)
-        cut = slice((1 - side) * half_tokens, (2 - side) * half_tokens)
-        same = slice(side * half_tokens, (side + 1) * half_tokens)
-        vout[side, same] = both[same].astype(BF16)
-        vout[side, cut] = (both[cut] + hin[1 - side].astype(F32)).astype(BF16)
-        v_copies.append(to_peer(k, vout.at[side], vin.at[side], v_send, v_recv.at[side]))
-        v_copies[-1].start()
-
+    for part in range(2):
+        cut = slice(part * half_tokens, (part + 1) * half_tokens)
+        for side, k in enumerate(SIDES):
+            last_copies[k, part].wait_recv()
+            ours = dot(oc[k, cut], w[...])
+            if part == 0:
+                to_partner[k + CORE].wait_recv()
+            ours = ours + pin[k // 2, cut].astype(F32)
+            if part != side:
+                halves[part].wait_recv()
+                ours = ours + hin[part].astype(F32)
+            vout[side, cut] = ours.astype(BF16)
+            v_copies.append(
+                to_peer(k, vout.at[side, parts[part]], vin.at[side, parts[part]], v_send, v_recv.at[side, part])
+            )
+            v_copies[-1].start()
     wait_bytes(sg.at[:3], c_recv.at[3])
     for k in (*SIDES, DIAGONAL):
         to_peer(CORE, sg.at[peer(k)], sg.at[peer(k)], c_send.at[3], c_recv.at[4]).start()
+    for k in SIDES:
+        take_gradient(k)
 
     def gradient_slab(a):
         rows = [grad[t, pl.ds(a, groups, stride=slabs), :] for t in tiles]
@@ -357,25 +409,16 @@
         mom[:, cut] = MOMENTUM_DECAY * mom[:, cut] + part
         return part
 
-    c_hi, c_lo = split_hi_lo(from_momentum + coefficients(keep_moment))
+    kept = doubled(from_momentum + coefficients(keep_moment))
     for a in range(slabs):
         cut = slice(a * width, (a + 1) * width)
-        left[0, :, cut] = mom[:, cut] - dot3(c_hi, c_lo, bh[a], bl[a])
-
-    s_hi, s_lo = split_hi_lo(shared)
-    for a in range(slabs):
-        product = dot3(s_hi, s_lo, bh[a], bl[a])
-        for t in tiles:
-            upd[t, pl.ds(a, groups, stride=slabs), :] = product[:, t * LANES : (t + 1) * LANES]
-    for t in tiles:
-        cut = slice(t * LANES, (t + 1) * LANES)
-        nw[:, cut] = rebuild_rows(w[:, cut], upd[t])
+        left[0, :, cut] = mom[:, cut] - expand(kept, a)
 
     wait_bytes(sg.at[:4], c_recv.at[4])
     mixed = dot(xa[...], sg[...].reshape(n * groups, bands))
-    mixed = jnp.concatenate([mixed[a * tokens : (a + 1) * tokens] for a in range(slabs)], 1)
-    hi, lo = split_hi_lo(mixed)
-    change = dot3(hi, lo, bh[...].reshape(slabs * bands, width), bl[...].reshape(slabs * bands, width))
+    mixed = jnp.concatenate([doubled(mixed[a * tokens : (a + 1) * tokens]) for a in range(slabs)], 1)
+    change = dot(mixed, bw[...].reshape(2 * slabs * bands, width))
+    change = change[:tokens] + change[tokens:]
     to_partner[CORE].wait_recv()
     base = even[0] + pin[0].astype(F32) - LEARNING_RATE * change
     for copy in v_copies:
@@ -430,8 +473,7 @@
             pltpu.VMEM((n, tokens, width), BF16),
             pltpu.VMEM((own_rows, width), BF16),
             pltpu.VMEM((groups, group_len), F32),
-            pltpu.VMEM((slabs, bands, width), BF16),
-            pltpu.VMEM((slabs, bands, width), BF16),
+            pltpu.VMEM((slabs, 2 * bands, width), BF16),
             pltpu.VMEM((group_len, 2 * bands), BF16),
             pltpu.VMEM((span, span), BF16),
             pltpu.VMEM((slabs * tokens, depth // slabs), BF16),
@@ -453,9 +495,9 @@
             pltpu.VMEM((reps, groups, bands), BF16),
             pltpu.VMEM((n, groups, bands), BF16),
             dma((6,)),
-            dma, dma((n,)), dma, dma((n,)), dma, dma((half,)), dma, dma((2,)), dma((2,)),
+            dma, dma((n,)), dma((2, 2)), dma, dma((n,)), dma, dma((half,)), dma, dma((2,)), dma((2, 2)),
             dma((4,)), dma((5,)),
-            regular, regular((max(reps - 2, 1),)),
+            regular, regular((reps - 1,)), regular,
         ],
         compiler_params=pltpu.CompilerParams(collective_id=0, has_side_effects=True),
     )(band_index.reshape(1, -1), inputs, out_grad, weight, momentum)

time: 31.7 us -> 30.5 us (0.962)
  Pallas kernels: 30.9 us -> 29.8 us
    pallas_call x1, Pallas kernels: 29.7 us -> 28.6 us  [fused_shards(): pl.pallas_call(functools.partial(kernel, n, reps), out_shape=(pltpu.VMEM(...]
where the time goes in v2:
time: 30.5 us; the launch traced here: 30.4 us
  Pallas kernels  29.8 us (98%)
  between operations  0.64 us (2%)
    pallas_call x1, Pallas kernels, fused_shards(): pl.pallas_call(functools.partial(kernel, n, reps), out_shape=(pltpu.VMEM(...  28.6 us
    pallas_call x1, Pallas kernels, fused_shards(): pl.pallas_call(store_kernel, out_shape=tuple((jax.ShapeDtypeStruct(a.shap...  1.2 us

profile of v2, /device:TPU:0, one launch (start us, length us, event | category | flops | bytes accessed | tf_op | source)
XLA Modules:
  0.0 30.4 jit_solution(7950518872680982480)
XLA Ops:
  0.6 28.6 %shard_map.76 = (f32[1,64,4096]{2,1,0:T(8,128)S(1)}, bf16[512,512]{1,0:T(8,128)(2,1)S(1)}, bf16[1,128,512]{2,1,0:T(8,128)(2,1)S(1)}) custom-call(s32[1,128]{1,0:T(1,128)} %bitcast.1, bf16[1,128,4096]{2,1,0:T(8,128)(2,1)} %x_hbm.1, bf16[1,128,512]{2,1,0:T(8,128)(2,1)} %og_hbm.1, bf16[512,512]{1,0:T(8,128)(2,1)} %w_hbm.1, f32[1,64,4096]{2,1,0:T(8,128)} %mom_hbm.1), custom_call_target="tpu_custom_call" | custom-call | tf_op jit(solution)/shard_map/pallas_call | solution.py:460
  29.2 1.2 %shard_map.77 = (f32[1,64,4096]{2,1,0:T(8,128)}, bf16[512,512]{1,0:T(8,128)(2,1)}, bf16[1,128,512]{2,1,0:T(8,128)(2,1)}) custom-call(f32[1,64,4096]{2,1,0:T(8,128)S(1)} %get-tuple-element.6.left, bf16[512,512]{1,0:T(8,128)(2,1)S(1)} %get-tuple-element.7.nw, bf16[1,128,512]{2,1,0:T(8,128)(2,1)S(1)} %get-tuple-element.8.val), custom_call_target="tpu_custom_call" | custom-call | tf_op jit(solution)/shard_map/pallas_call | solution.py:504

commit v3 on v2

--- a/solution.py
+++ b/solution.py
@@ -78,7 +78,7 @@
     return jnp.concatenate([jnp.concatenate([part, part], 1) for part in (hi, lo)], 0)
 
 
-def fill_basis(band_ref, bw, bt, between):
+def fill_basis(band_ref, bw, bt, before, beside):
     slabs, bands, width = bw.shape
     bands //= 2
     length = slabs * width
@@ -94,27 +94,33 @@
     fine, coarse = angle(2 * lane + 1), angle(2 * LANES * lane)
     cos_fine, sin_fine = row_scale * jnp.cos(fine), row_scale * jnp.sin(fine)
     cos_coarse, sin_coarse = jnp.cos(coarse), jnp.sin(coarse)
-    between()
-    for at in range(length // LANES):
+    turned = [part.T for part in (cos_fine, sin_fine, cos_coarse, sin_coarse)]
+    before()
+    tiles = length // LANES
+    for at in range(tiles):
         tile = cos_coarse[:, at : at + 1] * cos_fine - sin_coarse[:, at : at + 1] * sin_fine
         hi, lo = split_hi_lo(tile)
         a, col = divmod(at * LANES, width)
         bw[a, :bands, col : col + LANES] = hi
         bw[a, bands:, col : col + LANES] = lo
-        hi, lo = split_hi_lo(tile.T)
+        tile = turned[2][at : at + 1] * turned[0] - turned[3][at : at + 1] * turned[1]
+        hi, lo = split_hi_lo(tile)
         bt[at * LANES : (at + 1) * LANES, :bands] = hi
         bt[at * LANES : (at + 1) * LANES, bands:] = lo
+        beside(at, tiles)
 
 
 CORE, SIDES, DIAGONAL = 1, (2, 4), 6
+ARRIVALS = ((0, CORE), (DIAGONAL, DIAGONAL + CORE), tuple(k + CORE for k in SIDES), SIDES)
+PLACE = {k: i for i, k in enumerate(sum(ARRIVALS, ()))}
+LAST_STEPS = 4
 
 
 def kernel(
     n, reps, band_hbm, x_hbm, og_hbm, w_hbm, mom_hbm, left, nw, val,
     band, x, oc, og, w, mom, bw, bt, perm, xa, zc, grad, upd, even, odd, pin, vout, vin, hout, hin,
-    cl, cpo, cpi, cro, cri, cz, sg,
-    load_sem, x_send, x_recv, last_recv, og_send, og_recv, p_send, p_recv, v_send, h_recv, v_recv, c_send, c_recv,
-    side_entered, rep_round, all_entered,
+    cl, cpo, cpi, zo, zi, cx, sg,
+    load_sem, send_sem, x_recv, og_recv, p_recv, v_recv, c_recv, side_entered, rep_round, all_entered,
 ):
     me, rep = lax.axis_index("fsdp"), lax.axis_index("rep")
     tokens, depth = x.shape
@@ -146,6 +152,10 @@
     def wait_bytes(like, sem):
         pltpu.make_async_copy(like, like, sem).wait()
 
+    def wait_total(count, sem):
+        like = bt.at[: count // (2 * bt.shape[1])]
+        pltpu.make_async_copy(like, like, sem).wait()
+
     def signal_peer(sem, k):
         pl.semaphore_signal(sem, inc=1, device_id={"fsdp": peer(k)}, device_id_type=pl.DeviceIdType.MESH)
 
@@ -183,15 +193,13 @@
         signal_peer(barrier, k)
     loads = [
         pltpu.make_async_copy(src, dst, load_sem.at[i])
-        for i, (src, dst) in enumerate(
-            (
-                (band_hbm, band),
-                (x_hbm.at[0], x),
-                (og_hbm.at[0], og.at[0]),
-                (w_hbm, w),
-                (mom_hbm.at[0], mom),
-                (x_hbm.at[0, :, columns(me)], oc.at[0]),
-            )
+        for i, src, dst in (
+            (0, band_hbm, band),
+            (1, x_hbm.at[0], x),
+            (2, og_hbm.at[0], og.at[0]),
+            (3, w_hbm, w),
+            (3, mom_hbm.at[0], mom),
+            (3, x_hbm.at[0, :, columns(me)], oc.at[0]),
         )
     ]
     for load in loads:
@@ -199,28 +207,38 @@
     pl.semaphore_wait(barrier, len(near) + jnp.where(first, next_reps, 0))
 
     signal_peer(side_entered, SIDES[0])
-    og_copies = {k: to_peer(k, og_hbm.at[0], og.at[k], og_send, og_recv.at[k]) for k in (*SIDES, CORE)}
+    block = 2 * tokens * width
+    parts = [pl.ds(part * half_tokens, half_tokens) for part in range(2)]
+    x_sem = {CORE: 0, DIAGONAL: 1, DIAGONAL + CORE: 2, **{k + CORE: 3 for k in SIDES}}
+    og_sem = {CORE: 0, **{k: 1 for k in SIDES}, **{k + CORE: 2 for k in SIDES}, DIAGONAL + CORE: 4}
+    og_copies = {
+        k: to_peer(k, og_hbm.at[0], og.at[PLACE[k]], send_sem.at[0], og_recv.at[og_sem[k]]) for k in (*SIDES, CORE)
+    }
     x_copies = {
-        k: to_peer(k, x_hbm.at[0, :, columns(peer(k))], oc.at[k], x_send, x_recv.at[k])
-        for k in range(1, n)
-        if k not in SIDES
+        k: to_peer(
+            k, x_hbm.at[0, :, columns(peer(k))], oc.at[PLACE[k]], send_sem.at[0], x_recv.at[x_sem[k]]
+        )
+        for k in x_sem
     }
-    parts = [pl.ds(side * half_tokens, half_tokens) for side in range(2)]
-    last_copies = {
-        (k, part): to_peer(
-            k, x_hbm.at[0, parts[part], columns(peer(k))], oc.at[k, parts[part]], x_send, last_recv.at[i, part]
-        )
-        for i, k in enumerate(SIDES)
-        for part in range(2)
-    }
+    steps = [pl.ds(step * (tokens // LAST_STEPS), tokens // LAST_STEPS) for step in range(LAST_STEPS)]
+    last_copies = [
+        to_peer(
+            k, x_hbm.at[0, steps[step], columns(peer(k))], oc.at[PLACE[k], steps[step]],
+            send_sem.at[0], x_recv.at[4 + step],
+        )
+        for step in range(LAST_STEPS)
+        for k in SIDES
+    ]
     forward = {
-        k: to_peer(CORE, og.at[k], og.at[k + CORE], og_send, og_recv.at[k + CORE])
+        k: to_peer(
+            CORE, og.at[PLACE[k]], og.at[PLACE[k + CORE]], send_sem.at[0], og_recv.at[og_sem[k + CORE]]
+        )
         for k in (*SIDES, DIAGONAL)
     }
     relays = [
         to_peer(
-            SIDES[side], og.at[SIDES[1 - side], parts[side]], og.at[DIAGONAL, parts[side]],
-            og_send, og_recv.at[DIAGONAL],
+            SIDES[side], og.at[PLACE[SIDES[1 - side]], parts[side]], og.at[PLACE[DIAGONAL], parts[side]],
+            send_sem.at[0], og_recv.at[3],
         )
         for side in range(2)
     ]
@@ -228,27 +246,33 @@
         copy.start()
     x_copies[CORE].start()
 
-    def reach_diagonal():
+    span = slabs * LANES
+    pieces = depth // span
+
+    def before_tiles():
+        row = lax.broadcasted_iota(jnp.int32, (span, LANES), 0)
+        lane = lax.broadcasted_iota(jnp.int32, (span, LANES), 1)
+        for a in range(slabs):
+            perm[:, a * LANES : (a + 1) * LANES] = (row == slabs * lane + a).astype(F32).astype(BF16)
         pl.semaphore_wait(side_entered, 1)
         x_copies[DIAGONAL].start()
+        x_copies[DIAGONAL + CORE].start()
         signal_next_reps(rep_round.at[0])
 
-    loads[0].wait()
-    fill_basis(band, bw, bt, reach_diagonal)
-
-    pass_on(0)
-    loads[1].wait()
-    span = slabs * LANES
-    row = lax.broadcasted_iota(jnp.int32, (span, LANES), 0)
-    lane = lax.broadcasted_iota(jnp.int32, (span, LANES), 1)
-    for a in range(slabs):
-        perm[:, a * LANES : (a + 1) * LANES] = (row == slabs * lane + a).astype(F32).astype(BF16)
-    for piece in range(depth // span):
+    def sort_tokens(at, steps):
+        if (at + 1) * pieces % steps:
+            return
+        piece = (at + 1) * pieces // steps - 1
         sorted_piece = dot(x[:, piece * span : (piece + 1) * span], perm[...]).astype(BF16)
         for a in range(slabs):
             xa[a * tokens : (a + 1) * tokens, piece * LANES : (piece + 1) * LANES] = sorted_piece[
                 :, a * LANES : (a + 1) * LANES
             ]
+
+    loads[0].wait()
+    loads[1].wait()
+    fill_basis(band, bw, bt, before_tiles, sort_tokens)
+    pass_on(0)
 
     loads[2].wait()
     for a in range(slabs):
@@ -258,19 +282,19 @@
         zc[a * tokens : (a + 1) * tokens, bands:] = lo
     both = dot(xa[...], zc[...], ((0,), (0,)))
     cl[...] = (scaling * (both[:, :bands] + both[:, bands:])).reshape(n, groups, bands)
-    for h in range(n // 2):
-        cpo[h] = cl[peer(2 * h + CORE)].astype(BF16)
-    pair_copy = to_peer(CORE, cpo, cpi, c_send.at[0], c_recv.at[0])
+    core = lax.rem(me, 2)
+    for c in range(n // 2):
+        cpo[c] = cl[2 * c + 1 - core].astype(BF16)
+    pair_copy = to_peer(CORE, cpo, cpi, send_sem.at[2], c_recv.at[0])
     pair_copy.start()
 
     pass_on(1)
-    for k in SIDES:
-        og_copies[k].wait_recv()
+    wait_bytes(og.at[:2], og_recv.at[1])
     for copy in relays:
         copy.start()
     for k in SIDES:
         forward[k].start()
-
+        x_copies[k + CORE].start()
     def coefficients(slab_of):
         both = None
         for a in range(slabs):
@@ -280,161 +304,143 @@
         both = both[:, :bands] + both[:, bands:]
         return both[:groups] + both[groups:]
 
-    def expand(stacked, a):
-        both = dot(stacked, bw[a])
-        return both[:groups] + both[groups:]
-
-    for load in loads[3:]:
-        load.wait()
-    tiles = range(width // LANES)
-    product = dot(oc[0], og[0], ((0,), (0,)))
-    for t in tiles:
-        grad[t] = product[:, t * LANES : (t + 1) * LANES]
-    even[0] = dot(oc[0], w[...])
-    to_partner = {}
-
-    def take_values(k):
-        x_copies[k].wait_recv()
-        partial = dot(oc[k], w[...])
-        if k % 2:
-            odd[k // 2] = partial.astype(BF16)
-            to_partner[k] = to_peer(CORE, odd.at[k // 2], pin.at[k // 2], p_send, p_recv.at[k // 2])
-            to_partner[k].start()
-        else:
-            even[k // 2] = partial
-
-    def take_gradient(k):
-        if k == CORE:
-            og_copies[CORE].wait_recv()
-        elif k % 2:
-            forward[k - CORE].wait_recv()
-        product = dot(oc[k], og[k], ((0,), (0,)))
-        for t in tiles:
-            grad[t] += product[:, t * LANES : (t + 1) * LANES]
-
-    def take(k):
-        take_values(k)
-        take_gradient(k)
-
-    take(CORE)
-    pair_copy.wait_recv()
-    for h in range(1, n // 2):
-        cro[h] = (cl[peer(2 * h)] + cpi[h].astype(F32)).astype(BF16)
-        to_peer(2 * h, cro.at[h], cri.at[h], c_send.at[1], c_recv.at[1]).start()
+    wait_total(2 * own_rows * width + 4 * groups * slabs * width + 2 * tokens * own_rows, load_sem.at[3])
     from_momentum = coefficients(lambda a: MOMENTUM_DECAY * mom[:, a * width : (a + 1) * width])
-    own_sum = from_momentum + (cl[me] + cpi[0].astype(F32))
-    for k in (DIAGONAL + CORE, *(k + CORE for k in SIDES)):
-        x_copies[k].start()
+    cl[me] += from_momentum
     for at in range(2, reps - 1):
         pass_on(at)
-    take_values(DIAGONAL)
-    wait_bytes(cri.at[1 : n // 2], c_recv.at[1])
-    for h in range(1, n // 2):
-        own_sum = own_sum + cri[h].astype(F32)
-    cz[rep] = own_sum.astype(BF16)
+    pair_copy.wait_recv()
+    for c in range(n // 2):
+        cl[2 * c + core] += cpi[c].astype(F32)
+        zo[c] = cl[2 * c + core].astype(BF16)
 
     @pl.when(jnp.logical_not(first))
     def _():
         pl.semaphore_wait(all_entered, 1)
 
     for d in range(1, reps):
-        to_rep(d, cz.at[rep], cz.at[rep], c_send.at[2], c_recv.at[2]).start()
-
-    wait_bytes(og.at[DIAGONAL], og_recv.at[DIAGONAL])
-    forward[DIAGONAL].start()
-    take_gradient(DIAGONAL)
-    for k in SIDES:
-        last_copies[k, 0].start()
-    take(DIAGONAL + CORE)
-    to_partner[DIAGONAL + CORE].wait_recv()
+        to_rep(d, zo.at[lax.rem(rep + d, reps)], zi.at[rep], send_sem.at[2], c_recv.at[1]).start()
+
+    tiles = range(width // LANES)
+
+    def to_partner(k, which):
+        copy = to_peer(CORE, odd.at[k // 2], pin.at[k // 2], send_sem.at[1], p_recv.at[which])
+        copy.start()
+        return copy
+
+    def add_gradient(pair):
+        at = slice(2 * pair, 2 * pair + 2)
+        product = dot(
+            oc[at].reshape(2 * tokens, own_rows), og[at].reshape(2 * tokens, width), ((0,), (0,))
+        )
+        for t in tiles:
+            cut = product[:, t * LANES : (t + 1) * LANES]
+            grad[t] = cut if pair == 0 else grad[t] + cut
+
+    x_copies[CORE].wait_recv()
+    both = dot(oc[0:2].reshape(2 * tokens, own_rows), w[...])
+    even[0] = both[:tokens]
+    odd[0] = both[tokens:].astype(BF16)
+    from_core = to_partner(CORE, 0)
+    og_copies[CORE].wait_recv()
+    add_gradient(0)
+    x_copies[DIAGONAL].wait_recv()
+    even[DIAGONAL // 2] = dot(oc[PLACE[DIAGONAL]], w[...])
+    x_copies[DIAGONAL + CORE].wait_recv()
+    odd[DIAGONAL // 2] = dot(oc[PLACE[DIAGONAL + CORE]], w[...]).astype(BF16)
+    from_diagonal = to_partner(DIAGONAL + CORE, 1)
+    wait_bytes(zi.at[: reps - 1], c_recv.at[1])
+    plane_sum = cl[2 * rep + core]
+    for d in range(1, reps):
+        plane_sum = plane_sum + zi[lax.rem(rep + d, reps)].astype(F32)
+    cx[0] = plane_sum.astype(BF16)
+    for k in (*SIDES, DIAGONAL):
+        to_peer(k, cx.at[0], cx.at[k // 2], send_sem.at[2], c_recv.at[2]).start()
+    from_diagonal.wait_recv()
     across = even[DIAGONAL // 2] + pin[DIAGONAL // 2].astype(F32)
-    halves = []
     for side, k in enumerate(SIDES):
         hout[side] = across[side * half_tokens : (side + 1) * half_tokens].astype(BF16)
-        halves.append(to_peer(k, hout.at[side], hin.at[side], v_send, h_recv.at[side]))
-        halves[-1].start()
-    for k in SIDES:
-        last_copies[k, 1].start()
-    take(SIDES[0] + CORE)
-    take(SIDES[1] + CORE)
-
-    wait_bytes(cz.at[: reps - 1], c_recv.at[2])
-    shared = cz[0].astype(F32)
+        to_peer(k, hout.at[side], hin.at[side], send_sem.at[1], v_recv.at[0]).start()
+    for copy in last_copies:
+        copy.start()
+    wait_bytes(og.at[0], og_recv.at[3])
+    forward[DIAGONAL].start()
+    wait_bytes(oc.at[:2], x_recv.at[3])
+    at = slice(PLACE[SIDES[0] + CORE], PLACE[SIDES[1] + CORE] + 1)
+    both = dot(oc[at].reshape(2 * tokens, own_rows), w[...])
+    for side, k in enumerate(SIDES):
+        odd[k // 2] = both[side * tokens : (side + 1) * tokens].astype(BF16)
+        to_partner(k + CORE, 2)
+    wait_bytes(cx.at[1:], c_recv.at[2])
+    total = plane_sum
+    for h in range(1, n // 2):
+        total = total + cx[h].astype(F32)
+    mine = 2 * rep + core
+    sg[mine] = (total / reps).astype(BF16)
     for d in range(1, reps):
-        shared = shared + cz[d].astype(F32)
-    shared = shared / reps
-    sg[me] = shared.astype(BF16)
-    for k in (*SIDES, DIAGONAL):
-        to_peer(k, sg.at[me], sg.at[me], c_send.at[3], c_recv.at[3]).start()
-    to_peer(CORE, sg.at[me], sg.at[me], c_send.at[3], c_recv.at[4]).start()
-    agreed = doubled(shared)
+        to_rep(d, sg.at[mine], sg.at[mine], send_sem.at[2], c_recv.at[3]).start()
+    to_peer(CORE, sg.at[mine], sg.at[mine], send_sem.at[2], c_recv.at[4]).start()
+    forward[DIAGONAL].wait_recv()
+    add_gradient(1)
+    wait_bytes(og.at[:2], og_recv.at[2])
+    add_gradient(2)
+
+    wait_bytes(pin.at[:2], p_recv.at[2])
+    wait_bytes(hin, v_recv.at[0])
+    for step in range(LAST_STEPS):
+        rows = tokens // LAST_STEPS
+        cut = slice(step * rows, (step + 1) * rows)
+        part, within = divmod(step * rows, half_tokens)
+        wait_bytes(oc.at[:2, steps[0]], x_recv.at[4 + step])
+        for side, k in enumerate(SIDES):
+            ours = dot(oc[PLACE[k], cut], w[...]) + pin[k // 2, cut].astype(F32)
+            if part != side:
+                ours = ours + hin[part, within : within + rows].astype(F32)
+            vout[side, cut] = ours.astype(BF16)
+            to_peer(k, vout.at[side, steps[step]], vin.at[side, steps[step]], send_sem.at[1], v_recv.at[1]).start()
+    add_gradient(3)
+
+    def gradient_slab(a):
+        rows = [grad[t, pl.ds(a, groups, stride=slabs), :] for t in tiles]
+        return scaling * jnp.concatenate(rows, 1)
+
+    def keep_moment(a):
+        part = gradient_slab(a)
+        cut = slice(a * width, (a + 1) * width)
+        mom[:, cut] = MOMENTUM_DECAY * mom[:, cut] + part
+        return part
+
+    kept = doubled(from_momentum + coefficients(keep_moment))
+    wait_bytes(sg.at[: reps - 1], c_recv.at[3])
+    for d in range(1, reps):
+        slot = 2 * lax.rem(rep + d, reps) + core
+        to_peer(CORE, sg.at[slot], sg.at[slot], send_sem.at[2], c_recv.at[4]).start()
+    from_core.wait_recv()
     for a in range(slabs):
-        product = expand(agreed, a)
+        cut = slice(a * width, (a + 1) * width)
+        both = dot(kept, bw[a])
+        left[0, :, cut] = mom[:, cut] - (both[:groups] + both[groups:])
+    agreed = jnp.concatenate([sg[me]] * 2, 1)
+    for a in range(slabs):
+        product = dot(agreed, bw[a])
         for t in tiles:
             upd[t, pl.ds(a, groups, stride=slabs), :] = product[:, t * LANES : (t + 1) * LANES]
     for t in tiles:
         cut = slice(t * LANES, (t + 1) * LANES)
         nw[:, cut] = rebuild_rows(w[:, cut], upd[t])
-
-    v_copies = []
-    for part in range(2):
-        cut = slice(part * half_tokens, (part + 1) * half_tokens)
-        for side, k in enumerate(SIDES):
-            last_copies[k, part].wait_recv()
-            ours = dot(oc[k, cut], w[...])
-            if part == 0:
-                to_partner[k + CORE].wait_recv()
-            ours = ours + pin[k // 2, cut].astype(F32)
-            if part != side:
-                halves[part].wait_recv()
-                ours = ours + hin[part].astype(F32)
-            vout[side, cut] = ours.astype(BF16)
-            v_copies.append(
-                to_peer(k, vout.at[side, parts[part]], vin.at[side, parts[part]], v_send, v_recv.at[side, part])
-            )
-            v_copies[-1].start()
-    wait_bytes(sg.at[:3], c_recv.at[3])
-    for k in (*SIDES, DIAGONAL):
-        to_peer(CORE, sg.at[peer(k)], sg.at[peer(k)], c_send.at[3], c_recv.at[4]).start()
-    for k in SIDES:
-        take_gradient(k)
-
-    def gradient_slab(a):
-        rows = [grad[t, pl.ds(a, groups, stride=slabs), :] for t in tiles]
-        return scaling * jnp.concatenate(rows, 1)
-
-    def keep_moment(a):
-        part = gradient_slab(a)
-        cut = slice(a * width, (a + 1) * width)
-        mom[:, cut] = MOMENTUM_DECAY * mom[:, cut] + part
-        return part
-
-    kept = doubled(from_momentum + coefficients(keep_moment))
-    for a in range(slabs):
-        cut = slice(a * width, (a + 1) * width)
-        left[0, :, cut] = mom[:, cut] - expand(kept, a)
-
-    wait_bytes(sg.at[:4], c_recv.at[4])
-    mixed = dot(xa[...], sg[...].reshape(n * groups, bands))
-    mixed = jnp.concatenate([doubled(mixed[a * tokens : (a + 1) * tokens]) for a in range(slabs)], 1)
-    change = dot(mixed, bw[...].reshape(2 * slabs * bands, width))
-    change = change[:tokens] + change[tokens:]
-    to_partner[CORE].wait_recv()
+    wait_bytes(sg.at[: n // 2], c_recv.at[4])
+    mixed = dot(xa[...], sg[...].reshape(n * groups, bands)).astype(BF16)
+    mixed = [mixed[a * tokens : (a + 1) * tokens] for a in range(slabs) for _ in range(2)]
+    change = dot(jnp.concatenate(mixed, 1), bw[...].reshape(2 * slabs * bands, width))
     base = even[0] + pin[0].astype(F32) - LEARNING_RATE * change
-    for copy in v_copies:
-        copy.wait_recv()
+    wait_bytes(vin, v_recv.at[1])
     for side in range(2):
         base = base + vin[side].astype(F32)
     val[0] = (base * scaling).astype(BF16)
 
-    wait_bytes(oc.at[1:], x_send)
-    wait_bytes(og.at[1:], og_send)
-    wait_bytes(odd, p_send)
-    wait_bytes(odd.at[:3], v_send)
-    wait_bytes(cpo, c_send.at[0])
-    wait_bytes(cri.at[1:], c_send.at[1])
-    wait_bytes(cz.at[: reps - 1], c_send.at[2])
-    wait_bytes(sg.at[:7], c_send.at[3])
+    wait_total(14 * block, send_sem.at[0])
+    wait_total(7 * block, send_sem.at[1])
+    wait_total((3 * (n // 2) - 1 + 2 * (reps - 1)) * 2 * groups * bands, send_sem.at[2])
 
 
 def store_kernel(left, nw, val, left_hbm, nw_hbm, val_hbm, sems):
@@ -492,11 +498,9 @@
             pltpu.VMEM((half, groups, bands), BF16),
             pltpu.VMEM((half, groups, bands), BF16),
             pltpu.VMEM((half, groups, bands), BF16),
-            pltpu.VMEM((reps, groups, bands), BF16),
+            pltpu.VMEM((half, groups, bands), BF16),
             pltpu.VMEM((n, groups, bands), BF16),
-            dma((6,)),
-            dma, dma((n,)), dma((2, 2)), dma, dma((n,)), dma, dma((half,)), dma, dma((2,)), dma((2, 2)),
-            dma((4,)), dma((5,)),
+            dma((4,)), dma((3,)), dma((4 + LAST_STEPS,)), dma((5,)), dma((3,)), dma((2,)), dma((5,)),
             regular, regular((reps - 1,)), regular,
         ],
         compiler_params=pltpu.CompilerParams(collective_id=0, has_side_effects=True),
@@ -517,10 +521,11 @@
     groups, group_len = momentum.shape[1:]
     return (
         n == CORE + DIAGONAL + 1
-        and reps > 1
+        and reps == n // 2
         and group_len & (group_len - 1) == 0
-        and tokens % 32 == 0
+        and tokens % (16 * LAST_STEPS) == 0
         and own_rows % LANES == 0
+        and own_rows == width
         and width % LANES == 0
         and groups % 16 == 0
         and group_len % width == 0

time: 30.5 us -> 29.6 us (0.970)
  Pallas kernels: 29.8 us -> 28.8 us
    pallas_call x1, Pallas kernels: 28.6 us -> 27.6 us  [fused_shards(): pl.pallas_call(functools.partial(kernel, n, reps), out_shape=(pltpu.VMEM(...]
where the time goes in v3:
time: 29.6 us; the launch traced here: 29.5 us
  Pallas kernels  28.8 us (97%)
  between operations  0.64 us (2%)
    pallas_call x1, Pallas kernels, fused_shards(): pl.pallas_call(functools.partial(kernel, n, reps), out_shape=(pltpu.VMEM(...  27.6 us
    pallas_call x1, Pallas kernels, fused_shards(): pl.pallas_call(store_kernel, out_shape=tuple((jax.ShapeDtypeStruct(a.shap...  1.2 us

profile of v3, /device:TPU:0, one launch (start us, length us, event | category | flops | bytes accessed | tf_op | source)
XLA Modules:
  0.0 29.5 jit_solution(3741085553248334026)
XLA Ops:
  0.6 27.6 %shard_map.76 = (f32[1,64,4096]{2,1,0:T(8,128)S(1)}, bf16[512,512]{1,0:T(8,128)(2,1)S(1)}, bf16[1,128,512]{2,1,0:T(8,128)(2,1)S(1)}) custom-call(s32[1,128]{1,0:T(1,128)} %bitcast.1, bf16[1,128,4096]{2,1,0:T(8,128)(2,1)} %x_hbm.1, bf16[1,128,512]{2,1,0:T(8,128)(2,1)} %og_hbm.1, bf16[512,512]{1,0:T(8,128)(2,1)} %w_hbm.1, f32[1,64,4096]{2,1,0:T(8,128)} %mom_hbm.1), custom_call_target="tpu_custom_call" | custom-call | tf_op jit(solution)/shard_map/pallas_call | solution.py:466
  28.3 1.2 %shard_map.77 = (f32[1,64,4096]{2,1,0:T(8,128)}, bf16[512,512]{1,0:T(8,128)(2,1)}, bf16[1,128,512]{2,1,0:T(8,128)(2,1)}) custom-call(f32[1,64,4096]{2,1,0:T(8,128)S(1)} %get-tuple-element.6.left, bf16[512,512]{1,0:T(8,128)(2,1)S(1)} %get-tuple-element.7.nw, bf16[1,128,512]{2,1,0:T(8,128)(2,1)S(1)} %get-tuple-element.8.val), custom_call_target="tpu_custom_call" | custom-call | tf_op jit(solution)/shard_map/pallas_call | solution.py:508

commit v4 on v3

--- a/solution.py
+++ b/solution.py
@@ -120,7 +120,7 @@
     n, reps, band_hbm, x_hbm, og_hbm, w_hbm, mom_hbm, left, nw, val,
     band, x, oc, og, w, mom, bw, bt, perm, xa, zc, grad, upd, even, odd, pin, vout, vin, hout, hin,
     cl, cpo, cpi, zo, zi, cx, sg,
-    load_sem, send_sem, x_recv, og_recv, p_recv, v_recv, c_recv, side_entered, rep_round, all_entered,
+    load_sem, send_sem, x_recv, og_recv, p_recv, v_recv, c_recv, side_entered, next_entered, rep_round,
 ):
     me, rep = lax.axis_index("fsdp"), lax.axis_index("rep")
     tokens, depth = x.shape
@@ -159,36 +159,30 @@
     def signal_peer(sem, k):
         pl.semaphore_signal(sem, inc=1, device_id={"fsdp": peer(k)}, device_id_type=pl.DeviceIdType.MESH)
 
-    first = me == 0
-
-    def signal_next_reps(sem):
-        for there, step in ((rep > 0, -1), (rep < reps - 1, 1)):
-
-            @pl.when(first & there)
+    def signal_rep(sem, step):
+        @pl.when(rep > 0 if step < 0 else rep < reps - 1)
+        def _():
+            pl.semaphore_signal(sem, inc=1, device_id={"rep": rep + step}, device_id_type=pl.DeviceIdType.MESH)
+
+    below, above = (rep > 0).astype(jnp.int32), (rep < reps - 1).astype(jnp.int32)
+
+    def hear_reps(at):
+        if at == 0:
+
+            @pl.when(rep < reps - 1)
             def _():
-                pl.semaphore_signal(
-                    sem, inc=1, device_id={"rep": rep + step}, device_id_type=pl.DeviceIdType.MESH
-                )
-
-    next_reps = (rep > 0).astype(jnp.int32) + (rep < reps - 1).astype(jnp.int32)
-
-    def pass_on(at):
-        @pl.when(first)
-        def _():
-            pl.semaphore_wait(rep_round.at[at], next_reps)
-
-        if at + 1 < reps - 1:
-            signal_next_reps(rep_round.at[at + 1])
-            return
-        for k in range(1, n):
-
-            @pl.when(first)
-            def _():
-                signal_peer(all_entered, k)
+                pl.semaphore_wait(next_entered, 1)
+
+        else:
+            pl.semaphore_wait(rep_round.at[at - 1], below + above)
+        if at < reps - 2:
+            for step in (-1, 1):
+                signal_rep(rep_round.at[at], step)
 
     barrier = pltpu.get_barrier_semaphore()
+    core = lax.rem(me, 2)
     near = [CORE] + [k + c for k in SIDES for c in (0, CORE)]
-    signal_next_reps(barrier)
+    signal_rep(barrier, 1)
     for k in near:
         signal_peer(barrier, k)
     loads = [
@@ -204,9 +198,10 @@
     ]
     for load in loads:
         load.start()
-    pl.semaphore_wait(barrier, len(near) + jnp.where(first, next_reps, 0))
+    pl.semaphore_wait(barrier, len(near) + below)
 
     signal_peer(side_entered, SIDES[0])
+    signal_rep(next_entered, -1)
     block = 2 * tokens * width
     parts = [pl.ds(part * half_tokens, half_tokens) for part in range(2)]
     x_sem = {CORE: 0, DIAGONAL: 1, DIAGONAL + CORE: 2, **{k + CORE: 3 for k in SIDES}}
@@ -237,10 +232,11 @@
     }
     relays = [
         to_peer(
-            SIDES[side], og.at[PLACE[SIDES[1 - side]], parts[side]], og.at[PLACE[DIAGONAL], parts[side]],
+            SIDES[side] + c, og.at[PLACE[SIDES[1 - side] + c], parts[side]], og.at[PLACE[DIAGONAL], parts[side]],
             send_sem.at[0], og_recv.at[3],
         )
         for side in range(2)
+        for c in (0, CORE)
     ]
     for copy in og_copies.values():
         copy.start()
@@ -257,7 +253,6 @@
         pl.semaphore_wait(side_entered, 1)
         x_copies[DIAGONAL].start()
         x_copies[DIAGONAL + CORE].start()
-        signal_next_reps(rep_round.at[0])
 
     def sort_tokens(at, steps):
         if (at + 1) * pieces % steps:
@@ -272,7 +267,7 @@
     loads[0].wait()
     loads[1].wait()
     fill_basis(band, bw, bt, before_tiles, sort_tokens)
-    pass_on(0)
+    hear_reps(0)
 
     loads[2].wait()
     for a in range(slabs):
@@ -282,16 +277,13 @@
         zc[a * tokens : (a + 1) * tokens, bands:] = lo
     both = dot(xa[...], zc[...], ((0,), (0,)))
     cl[...] = (scaling * (both[:, :bands] + both[:, bands:])).reshape(n, groups, bands)
-    core = lax.rem(me, 2)
     for c in range(n // 2):
         cpo[c] = cl[2 * c + 1 - core].astype(BF16)
     pair_copy = to_peer(CORE, cpo, cpi, send_sem.at[2], c_recv.at[0])
     pair_copy.start()
 
-    pass_on(1)
+    hear_reps(1)
     wait_bytes(og.at[:2], og_recv.at[1])
-    for copy in relays:
-        copy.start()
     for k in SIDES:
         forward[k].start()
         x_copies[k + CORE].start()
@@ -308,16 +300,11 @@
     from_momentum = coefficients(lambda a: MOMENTUM_DECAY * mom[:, a * width : (a + 1) * width])
     cl[me] += from_momentum
     for at in range(2, reps - 1):
-        pass_on(at)
+        hear_reps(at)
     pair_copy.wait_recv()
     for c in range(n // 2):
         cl[2 * c + core] += cpi[c].astype(F32)
         zo[c] = cl[2 * c + core].astype(BF16)
-
-    @pl.when(jnp.logical_not(first))
-    def _():
-        pl.semaphore_wait(all_entered, 1)
-
     for d in range(1, reps):
         to_rep(d, zo.at[lax.rem(rep + d, reps)], zi.at[rep], send_sem.at[2], c_recv.at[1]).start()
 
@@ -344,11 +331,13 @@
     from_core = to_partner(CORE, 0)
     og_copies[CORE].wait_recv()
     add_gradient(0)
-    x_copies[DIAGONAL].wait_recv()
-    even[DIAGONAL // 2] = dot(oc[PLACE[DIAGONAL]], w[...])
-    x_copies[DIAGONAL + CORE].wait_recv()
-    odd[DIAGONAL // 2] = dot(oc[PLACE[DIAGONAL + CORE]], w[...]).astype(BF16)
-    from_diagonal = to_partner(DIAGONAL + CORE, 1)
+    wait_bytes(og.at[:2], og_recv.at[2])
+
+    @pl.when(core == 1)
+    def _():
+        for copy in relays:
+            copy.start()
+
     wait_bytes(zi.at[: reps - 1], c_recv.at[1])
     plane_sum = cl[2 * rep + core]
     for d in range(1, reps):
@@ -356,6 +345,11 @@
     cx[0] = plane_sum.astype(BF16)
     for k in (*SIDES, DIAGONAL):
         to_peer(k, cx.at[0], cx.at[k // 2], send_sem.at[2], c_recv.at[2]).start()
+    x_copies[DIAGONAL].wait_recv()
+    even[DIAGONAL // 2] = dot(oc[PLACE[DIAGONAL]], w[...])
+    x_copies[DIAGONAL + CORE].wait_recv()
+    odd[DIAGONAL // 2] = dot(oc[PLACE[DIAGONAL + CORE]], w[...]).astype(BF16)
+    from_diagonal = to_partner(DIAGONAL + CORE, 1)
     from_diagonal.wait_recv()
     across = even[DIAGONAL // 2] + pin[DIAGONAL // 2].astype(F32)
     for side, k in enumerate(SIDES):
@@ -363,8 +357,6 @@
         to_peer(k, hout.at[side], hin.at[side], send_sem.at[1], v_recv.at[0]).start()
     for copy in last_copies:
         copy.start()
-    wait_bytes(og.at[0], og_recv.at[3])
-    forward[DIAGONAL].start()
     wait_bytes(oc.at[:2], x_recv.at[3])
     at = slice(PLACE[SIDES[0] + CORE], PLACE[SIDES[1] + CORE] + 1)
     both = dot(oc[at].reshape(2 * tokens, own_rows), w[...])
@@ -380,10 +372,11 @@
     for d in range(1, reps):
         to_rep(d, sg.at[mine], sg.at[mine], send_sem.at[2], c_recv.at[3]).start()
     to_peer(CORE, sg.at[mine], sg.at[mine], send_sem.at[2], c_recv.at[4]).start()
+    wait_bytes(og.at[0], og_recv.at[3])
+    forward[DIAGONAL].start()
+    add_gradient(2)
     forward[DIAGONAL].wait_recv()
     add_gradient(1)
-    wait_bytes(og.at[:2], og_recv.at[2])
-    add_gradient(2)
 
     wait_bytes(pin.at[:2], p_recv.at[2])
     wait_bytes(hin, v_recv.at[0])
@@ -438,7 +431,12 @@
         base = base + vin[side].astype(F32)
     val[0] = (base * scaling).astype(BF16)
 
-    wait_total(14 * block, send_sem.at[0])
+    for value, blocks in ((0, 13), (1, 15)):
+
+        @pl.when(core == value)
+        def _():
+            wait_total(blocks * block, send_sem.at[0])
+
     wait_total(7 * block, send_sem.at[1])
     wait_total((3 * (n // 2) - 1 + 2 * (reps - 1)) * 2 * groups * bands, send_sem.at[2])
 
@@ -501,7 +499,7 @@
             pltpu.VMEM((half, groups, bands), BF16),
             pltpu.VMEM((n, groups, bands), BF16),
             dma((4,)), dma((3,)), dma((4 + LAST_STEPS,)), dma((5,)), dma((3,)), dma((2,)), dma((5,)),
-            regular, regular((reps - 1,)), regular,
+            regular, regular, regular((reps - 2,)),
         ],
         compiler_params=pltpu.CompilerParams(collective_id=0, has_side_effects=True),
     )(band_index.reshape(1, -1), inputs, out_grad, weight, momentum)
@@ -521,7 +519,7 @@
     groups, group_len = momentum.shape[1:]
     return (
         n == CORE + DIAGONAL + 1
-        and reps == n // 2
+        and reps == n // 2 > 2
         and group_len & (group_len - 1) == 0
         and tokens % (16 * LAST_STEPS) == 0
         and own_rows % LANES == 0

time: 29.6 us -> 29.3 us (0.990)
  Pallas kernels: 28.8 us -> 28.5 us
where the time goes in v4:
time: 29.3 us; the launch traced here: 29.2 us
  Pallas kernels  28.5 us (97%)
  between operations  0.64 us (2%)
    pallas_call x1, Pallas kernels, fused_shards(): pl.pallas_call(functools.partial(kernel, n, reps), out_shape=(pltpu.VMEM(...  27.3 us
    pallas_call x1, Pallas kernels, fused_shards(): pl.pallas_call(store_kernel, out_shape=tuple((jax.ShapeDtypeStruct(a.shap...  1.2 us

profile of v4, /device:TPU:0, one launch (start us, length us, event | category | flops | bytes accessed | tf_op | source)
XLA Modules:
  0.0 29.2 jit_solution(2953369293740744154)
XLA Ops:
  0.6 27.3 %shard_map.76 = (f32[1,64,4096]{2,1,0:T(8,128)S(1)}, bf16[512,512]{1,0:T(8,128)(2,1)S(1)}, bf16[1,128,512]{2,1,0:T(8,128)(2,1)S(1)}) custom-call(s32[1,128]{1,0:T(1,128)} %bitcast.1, bf16[1,128,4096]{2,1,0:T(8,128)(2,1)} %x_hbm.1, bf16[1,128,512]{2,1,0:T(8,128)(2,1)} %og_hbm.1, bf16[512,512]{1,0:T(8,128)(2,1)} %w_hbm.1, f32[1,64,4096]{2,1,0:T(8,128)} %mom_hbm.1), custom_call_target="tpu_custom_call" | custom-call | tf_op jit(solution)/shard_map/pallas_call | solution.py:464
  28.0 1.2 %shard_map.77 = (f32[1,64,4096]{2,1,0:T(8,128)}, bf16[512,512]{1,0:T(8,128)(2,1)}, bf16[1,128,512]{2,1,0:T(8,128)(2,1)}) custom-call(f32[1,64,4096]{2,1,0:T(8,128)S(1)} %get-tuple-element.6.left, bf16[512,512]{1,0:T(8,128)(2,1)S(1)} %get-tuple-element.7.nw, bf16[1,128,512]{2,1,0:T(8,128)(2,1)S(1)} %get-tuple-element.8.val), custom_call_target="tpu_custom_call" | custom-call | tf_op jit(solution)/shard_map/pallas_call | solution.py:506
